TPU v7x, 32 devices: a whole 2x2x4 slice. The times are simulated.
32 devices in a mesh: dom: 8 (over y, x, core), rep: 4 (over z).
Axes of the slice: x: 2, y: 2, z: 4, core: 2. Of those that a mesh axis runs over, the one named last changes fastest.
Arguments:
- features: bfloat16 [32768, 512], P(('dom', 'rep')), may hold values from -6 to 6
- w_self: bfloat16 [512, 512], replicated, may hold values from -0.25 to 0.25
- w_neigh: bfloat16 [512, 512], replicated, may hold values from -0.25 to 0.25
- local_tiles: bfloat16 [4096, 128, 128], P(('dom', 'rep')), may hold values from -0.09375 to 0.09375
- local_rows: int32 [4096], P(('dom', 'rep')), may hold values from 0 to 7
- local_cols: int32 [4096], P(('dom', 'rep')), may hold values from 0 to 31
- halo_tiles: bfloat16 [3072, 128, 128], P(('dom', 'rep')), may hold values from -0.09375 to 0.09375
- halo_rows: int32 [3072], P(('dom', 'rep')), may hold values from 0 to 7
- halo_cols: int32 [3072], P(('dom', 'rep')), may hold values from 0 to 3
- cut_rows: int32 [8, 4, 8, 64], P('dom', 'rep'), may hold values from 0 to 1023
- cut_counts: int32 [8, 4, 8], P('dom', 'rep'), may hold values from 0 to 64, as said below
- cotangent: bfloat16 [32768, 512], P(('dom', 'rep')), may hold values from -6 to 6
Outputs:
- out: bfloat16 [32768, 512], P(('dom', 'rep'))
- d_x: bfloat16 [32768, 512], P(('dom', 'rep'))
- d_w_self: float32 [512, 512], P('rep')
- d_w_neigh: float32 [512, 512], P('rep')
Inputs may be any that keep to these rules, and one draw needn't show every extreme that they name: Each device sends 64 rows to at least one partition and none to its own partition; slots from cut_counts[p, r, q] on are unused.
All inputs are finite; a program needn't handle non-finite values.
Results may differ from a plain program's by a relative error of at most 0.008.
Values may be sent and summed in bfloat16 or wider, within the bound.
No kernel may reach another device: no remote copies, remote signals or barrier semaphores. Data moves between devices by JAX's collectives and lax.ppermute only.
A program may use at most 128 MiB of HBM per device.

v0:
```python
import math

import jax
import jax.numpy as jnp
from jax import lax
from jax.experimental import pallas as pl
from jax.experimental.pallas import tpu as pltpu
from jax.sharding import PartitionSpec as P


ROW_STEP = 256


def densify_kernel(
    local_rows, local_cols, halo_rows, halo_cols, local_ref, halo_ref, dense_ref, hdense_ref, acc, hacc
):
    tile_size = local_ref.shape[1]

    def place(rows, cols, tiles, total):
        total[...] = jnp.zeros_like(total)

        def step(k, carry):
            row = pl.multiple_of(rows[k] * tile_size, tile_size)
            col = pl.multiple_of(cols[k] * tile_size, tile_size)
            total[pl.ds(row, tile_size), pl.ds(col, tile_size)] += tiles[k].astype(jnp.float32)
            return carry

        lax.fori_loop(0, tiles.shape[0], step, 0)

    place(local_rows, local_cols, local_ref, acc)
    dense_ref[...] = acc[...].astype(dense_ref.dtype)
    place(halo_rows, halo_cols, halo_ref, hacc)
    hdense_ref[...] = hacc[...].astype(hdense_ref.dtype)


def densify(local_tiles, local_rows, local_cols, halo_tiles, halo_rows, halo_cols, rows, cols, hcols):
    smem = pl.BlockSpec(memory_space=pltpu.SMEM)
    vmem = pl.BlockSpec(memory_space=pltpu.VMEM)
    return pl.pallas_call(
        densify_kernel,
        out_shape=(
            jax.ShapeDtypeStruct((rows, cols), jnp.bfloat16),
            jax.ShapeDtypeStruct((rows, hcols), jnp.bfloat16),
        ),
        in_specs=[smem] * 4 + [vmem] * 2,
        out_specs=(vmem, vmem),
        scratch_shapes=[pltpu.VMEM((rows, cols), jnp.float32), pltpu.VMEM((rows, hcols), jnp.float32)],
        compiler_params=pltpu.CompilerParams(vmem_limit_bytes=60 << 20),
        cost_estimate=pl.CostEstimate(
            flops=rows * cols * 2, bytes_accessed=rows * (cols + hcols) * 4, transcendentals=0
        ),
        name="densify",
    )(local_rows, local_cols, halo_rows, halo_cols, local_tiles, halo_tiles)


def dot(a, b):
    return jnp.dot(a, b, preferred_element_type=jnp.float32)


def dot_t(a, b):
    return lax.dot_general(a, b, (((0,), (0,)), ((), ())), preferred_element_type=jnp.float32)


def middle_kernel(
    acc_ref, dense_ref, outer_ref, inner_ref, pre_ref, cot_ref, w_ref,
    out_ref, neighbour_ref, grad_ref, agg_ref, term_ref, total, far,
):
    step = pl.program_id(0)

    @pl.when(step == 0)
    def _():
        far[...] = outer_ref[...] + inner_ref[...]

    dense = dense_ref[...]
    neighbour = (acc_ref[...] + dot(dense, far[...])).astype(jnp.bfloat16)
    neighbour_ref[...] = neighbour
    preact = pre_ref[...] + dot(neighbour, w_ref[...])
    sigmoid_pre = jax.nn.sigmoid(preact)
    out_ref[...] = (preact * sigmoid_pre).astype(out_ref.dtype)
    slope = sigmoid_pre * (1.0 + preact * (1.0 - sigmoid_pre))
    grad = (cot_ref[...].astype(jnp.float32) * slope).astype(jnp.bfloat16)
    grad_ref[...] = grad
    agg = lax.dot_general(
        grad, w_ref[...], (((1,), (1,)), ((), ())), preferred_element_type=jnp.float32
    ).astype(jnp.bfloat16)
    agg_ref[...] = agg
    term = dot_t(dense, agg)

    @pl.when(step == 0)
    def _():
        total[...] = term

    @pl.when(step > 0)
    def _():
        total[...] += term

    @pl.when(step == pl.num_programs(0) - 1)
    def _():
        term_ref[...] = total[...].astype(term_ref.dtype)


def middle(acc, dense, slot, outer, inner, pre_self, cotangent, w_neigh):
    rows, width = acc.shape
    step = math.gcd(rows, ROW_STEP)
    by_rows = pl.BlockSpec((step, width), lambda i: (i, 0))
    like = jax.ShapeDtypeStruct((rows, width), jnp.bfloat16)
    return pl.pallas_call(
        middle_kernel,
        grid=(rows // step,),
        out_shape=(like,) * 5,
        in_specs=[
            by_rows,
            pl.BlockSpec((step, rows), lambda i: (i, slot)),
            pl.BlockSpec((rows, width), lambda i: (0, 0)),
            pl.BlockSpec((rows, width), lambda i: (0, 0)),
            by_rows,
            by_rows,
            pl.BlockSpec(w_neigh.shape, lambda i: (0, 0)),
        ],
        out_specs=(by_rows,) * 4 + (pl.BlockSpec((rows, width), lambda i: (0, 0)),),
        scratch_shapes=[pltpu.VMEM((rows, width), jnp.float32), pltpu.VMEM((rows, width), jnp.bfloat16)],
        compiler_params=pltpu.CompilerParams(vmem_limit_bytes=40 << 20),
        cost_estimate=pl.CostEstimate(
            flops=4 * rows * width * (rows + width), bytes_accessed=18 << 20, transcendentals=rows * width
        ),
        name="middle",
    )(acc, dense, outer, inner, pre_self, cotangent, w_neigh)


def per_device(
    features,
    w_self,
    w_neigh,
    local_tiles,
    local_rows,
    local_cols,
    halo_tiles,
    halo_rows,
    halo_cols,
    cut_rows,
    cut_counts,
    cotangent,
):
    row_count, width = features.shape
    tile_size = local_tiles.shape[1]
    n = lax.axis_size("rep")
    dom = lax.axis_size("dom")
    me = lax.axis_index("rep")
    blocks = row_count // tile_size
    assert n == 4
    swap_one = [(0, 1), (1, 0), (2, 3), (3, 2)]
    swap_two = [(0, 2), (1, 3), (2, 0), (3, 1)]
    swap_inner = [(1, 2), (2, 1)]
    outward, inward = [(1, 0), (2, 3)], [(0, 1), (3, 2)]

    def move(value, pairs):
        return lax.ppermute(value, "rep", pairs)

    second = move(features, swap_two)
    first = move(features, swap_one)
    inner = move(features, swap_inner)

    slot = jnp.bitwise_xor(local_cols // blocks, me)
    slot_cols = slot * blocks + local_cols % blocks
    cut_list = cut_rows[0, 0]
    halo_size = cut_list.shape[0] * cut_list.shape[1]
    dense, hdense = densify(
        local_tiles,
        local_rows,
        slot_cols,
        halo_tiles,
        halo_rows,
        halo_cols,
        row_count,
        n * row_count,
        halo_size,
    )

    def part(slot_id):
        return dense[:, slot_id * row_count : (slot_id + 1) * row_count]

    slot_index = jnp.arange(cut_list.shape[1], dtype=jnp.int32)
    live = slot_index[None, :] < cut_counts[0, 0][:, None]
    node_ids = jnp.arange(row_count, dtype=jnp.int32)
    selector = (
        (cut_list.reshape(-1)[:, None] == node_ids[None, :]) & live.reshape(-1)[:, None]
    ).astype(jnp.bfloat16)
    chosen = dot(selector, features).astype(jnp.bfloat16)
    incoming = lax.all_to_all(
        chosen.reshape(dom, -1, width), "dom", split_axis=0, concat_axis=0, tiled=True
    ).reshape(halo_size, width)

    pre_self = dot(features, w_self)
    summed = dot(part(0), features) + dot(hdense, incoming)
    third = move(second, outward)
    summed = summed + dot(part(1), first)
    summed = summed + dot(part(2), second)
    out, neighbour, grad_pre, grad_agg, term = middle(
        summed, dense, 3, third, inner, pre_self, cotangent, w_neigh
    )

    passed = move(term, inward)
    near = move(term, swap_inner)

    grad_scale = float(row_count * n * dom) ** (-0.5)
    share = width // (n * dom)
    d_self = (dot_t(features, grad_pre) * grad_scale).astype(jnp.bfloat16)
    d_neigh = (dot_t(neighbour, grad_pre) * grad_scale).astype(jnp.bfloat16)
    halo_back = dot_t(hdense, grad_agg).astype(jnp.bfloat16)
    both = jnp.stack([d_self, d_neigh]).reshape(2, n, dom, share, width)
    both = jnp.transpose(both, (2, 1, 0, 3, 4)).reshape(dom, 2 * n * share, width)
    both = jnp.concatenate([halo_back.reshape(dom, -1, width), both], axis=1)
    both = lax.all_to_all(both, "dom", split_axis=0, concat_axis=0, tiled=True)
    slots = cut_list.shape[1]
    returned = both[:, :slots].reshape(halo_size, width)
    both = jnp.sum(both[:, slots:].astype(jnp.float32), axis=0).reshape(n, 2, share, width)
    both = lax.all_to_all(both, "rep", split_axis=0, concat_axis=0, tiled=True)
    both = jnp.sum(both, axis=0)
    both = lax.all_to_all(
        jnp.broadcast_to(both[None], (dom, 2, share, width)),
        "dom",
        split_axis=0,
        concat_axis=0,
        tiled=True,
    )
    d_w_self = both[:, 0].reshape(width // n, width)
    d_w_neigh = both[:, 1].reshape(width // n, width)

    one_term = dot_t(part(1), grad_agg).astype(jnp.bfloat16)
    one = move(one_term, swap_one)
    two_term = lax.optimization_barrier(dot_t(part(2), grad_agg))
    two_term = (two_term + passed.astype(jnp.float32)).astype(jnp.bfloat16)
    half = row_count // 2
    two_a = move(two_term[:half], swap_two)
    two_b = move(two_term[half:], swap_two)

    d_x = dot(grad_pre, w_self.T) + dot_t(part(0), grad_agg)
    d_x = d_x + dot_t(selector, returned)
    d_x = d_x + near.astype(jnp.float32) + one.astype(jnp.float32)
    d_x = lax.optimization_barrier(d_x)
    d_x = jnp.concatenate(
        [
            (d_x[:half] + two_a.astype(jnp.float32)).astype(jnp.bfloat16),
            (d_x[half:] + two_b.astype(jnp.float32)).astype(jnp.bfloat16),
        ]
    )
    return (out, d_x, d_w_self, d_w_neigh)


def solution(mesh):
    lead = ("dom", "rep")
    in_specs = (
        P(lead, None),
        P(),
        P(),
        P(lead, None, None),
        P(lead),
        P(lead),
        P(lead, None, None),
        P(lead),
        P(lead),
        P("dom", "rep", None, None),
        P("dom", "rep", None),
        P(lead, None),
    )
    out_specs = (P(lead, None), P(lead, None), P("rep", None), P("rep", None))

    return jax.shard_map(per_device, mesh=mesh, in_specs=in_specs, out_specs=out_specs, check_vma=False)
```

profile of v0, /device:TPU:0, one launch (start us, length us, event | category | flops | bytes accessed | tf_op | source)
XLA Modules:
  0.0 183.9 jit_solution(12445336172552280339)
XLA Ops:
  0.6 3.1 %collective-permute-start = (bf16[1024,512]{1,0:T(8,128)(2,1)}, bf16[1024,512]{1,0:T(8,128)(2,1)}, u32[]{:S(2)}, u32[]{:S(2)}) collective-permute-start(bf16[1024,512]{1,0:T(8,128)(2,1)} %param.12), channel_id=1, source_target_pairs={{0,1},{1,0},{2,3},{3,2},{4,5},{5,4},{6,7},{7,6},{8,9},{9,8},{10,11... | collective-permute-start | bytes 3145736 | tf_op jit(solution)/shard_map/ppermute | solution.py:157
  3.8 2.6 %collective-permute-start.1 = (bf16[1024,512]{1,0:T(8,128)(2,1)}, bf16[1024,512]{1,0:T(8,128)(2,1)}, u32[]{:S(2)}, u32[]{:S(2)}) collective-permute-start(bf16[1024,512]{1,0:T(8,128)(2,1)} %param.12), channel_id=1, source_target_pairs={{0,2},{1,3},{2,0},{3,1},{4,6},{5,7},{6,4},{7,5},{8,10},{9,11},{10,... | collective-permute-start | bytes 3145736 | tf_op jit(solution)/shard_map/ppermute | solution.py:157
  6.4 1.6 collective-permute-start.3
  9.6 2.8 %fusion.22 = bf16[512,512]{1,0:T(8,128)(2,1)} fusion(bf16[1024,512]{1,0:T(8,128)(2,1)} %param.12, s32[512]{0:T(512)S(1)} %eq.17, pred[512]{0:T(512)(128)(4,1)S(1)} %lt.33), kind=kOutput, calls=%fused_computation.26 | convolution fusion | flops 538181632 | bytes 1575424 | tf_op jit(solution)/shard_map/dot_general | solution.py:57
  12.3 3.7 %all-to-all-start = ((bf16[8,64,512]{2,1,0:T(8,128)(2,1)}), bf16[8,64,512]{2,1,0:T(8,128)(2,1)S(1)}, u32[]{:S(2)}, u32[]{:S(2)}) async-start(bf16[8,64,512]{2,1,0:T(8,128)(2,1)} %bitcast.1), calls=%async_computation | async-start | bytes 1048576 | tf_op jit(solution)/shard_map/all_to_all | solution.py:189
  16.1 1.9 %fusion.37.pre_ref = f32[1024,512]{1,0:T(8,128)S(1)} fusion(bf16[1024,512]{1,0:T(8,128)(2,1)} %param.12, bf16[512,512]{1,0:T(8,128)(2,1)S(1)} %copy-done), kind=kOutput, calls=%fused_computation.48 | convolution fusion | flops 536870912 | bytes 3670016 | tf_op jit(solution)/shard_map/dot_general | solution.py:57
  18.6 12.7 %densify.1 = (bf16[1024,4096]{1,0:T(8,128)(2,1)}, bf16[1024,512]{1,0:T(8,128)(2,1)}) custom-call(s32[128]{0:T(128)} %local_rows.1, s32[128]{0:T(128)} %fusion.33.local_cols, s32[96]{0:T(128)} %halo_rows.1, s32[96]{0:T(128)} %halo_cols.1, bf16[128,128,128]{2,1,0:T(8,128)(2,1)} %local_ref.1, bf16[96,128,128]{2,1,0:T(8,128)(2,1)} %halo_ref.1), custom_call_target="tpu_custom_call" | custom-call | flops 8388608 | bytes 18874368 | tf_op jit(solution)/shard_map/densify/pallas_call | solution.py:39
  31.2 4.5 %fusion.15 = f32[1024,512]{1,0:T(8,128)} fusion(bf16[1024,512]{1,0:T(8,128)(2,1)} %param.12, bf16[1024,4096]{1,0:T(8,128)(2,1)} %get-tuple-element.11.dense_ref), kind=kOutput, calls=%fused_computation.18 | convolution fusion | flops 1073741824 | bytes 5242880 | tf_op jit(solution)/shard_map/dot_general | solution.py:57
  35.7 17.7 %collective-permute-done.1 = bf16[1024,512]{1,0:T(8,128)(2,1)} collective-permute-done((bf16[1024,512]{1,0:T(8,128)(2,1)}, bf16[1024,512]{1,0:T(8,128)(2,1)}, u32[]{:S(2)}, u32[]{:S(2)}) %collective-permute-start.1) | collective-permute-done | bytes 1048608 | tf_op jit(solution)/shard_map/ppermute | solution.py:157
  54.8 1.9 %fusion.36 = f32[1024,512]{1,0:T(8,128)S(1)} fusion(bf16[1024,512]{1,0:T(8,128)(2,1)} %get-tuple-element.12, bf16[512,512]{1,0:T(8,128)(2,1)S(1)} %bitcast.38), kind=kOutput, calls=%fused_computation.47 | convolution fusion | flops 536870912 | bytes 3670016 | tf_op jit(solution)/shard_map/dot_general | solution.py:57
  56.7 3.3 %fusion.11 = f32[1024,512]{1,0:T(8,128)S(1)} fusion(bf16[1024,512]{1,0:T(8,128)(2,1)} %collective-permute-done, bf16[1024,4096]{1,0:T(8,128)(2,1)} %get-tuple-element.11.dense_ref), kind=kOutput, calls=%fused_computation.14 | convolution fusion | flops 1073741824 | bytes 5242880 | tf_op jit(solution)/shard_map/dot_general | solution.py:57
  60.0 3.2 %add_add_fusion.acc_ref = f32[1024,512]{1,0:T(8,128)S(1)} fusion(f32[1024,512]{1,0:T(8,128)S(1)} %fusion.11, f32[1024,512]{1,0:T(8,128)S(1)} %copy-done.8, f32[1024,512]{1,0:T(8,128)S(1)} %fusion.36, bf16[1024,512]{1,0:T(8,128)(2,1)} %collective-permute-done.1, bf16[1024,4096]{1,0:T(8,128)(2,1)} %get-tuple-element.11.dense_ref), kind=kOutput, calls=%fused_computation.3 | convolution fusion | flops 1075314688 | bytes 11534336 | tf_op jit(solution)/shard_map/dot_general | solution.py:57
  63.3 13.1 %collective-permute-done.2.outer_ref = bf16[1024,512]{1,0:T(8,128)(2,1)} collective-permute-done((bf16[1024,512]{1,0:T(8,128)(2,1)}, bf16[1024,512]{1,0:T(8,128)(2,1)}, u32[]{:S(2)}, u32[]{:S(2)}) %collective-permute-start.2) | collective-permute-done | bytes 1048608 | tf_op jit(solution)/shard_map/ppermute | solution.py:157
  76.4 9.4 %middle.1 = (bf16[1024,512]{1,0:T(8,128)(2,1)}, bf16[1024,512]{1,0:T(8,128)(2,1)S(1)}, bf16[1024,512]{1,0:T(8,128)(2,1)S(1)}, bf16[1024,512]{1,0:T(8,128)(2,1)S(1)}, bf16[1024,512]{1,0:T(8,128)(2,1)}) custom-call(f32[1024,512]{1,0:T(8,128)S(1)} %add_add_fusion.acc_ref, bf16[1024,4096]{1,0:T(8,128)(2,1)} %get-tuple-element.11.dense_ref, ...), custom_call_target="tpu_custom_call" | custom-call | flops 3221225472 | bytes 18874368 | tf_op jit(solution)/shard_map/middle/pallas_call | solution.py:107
  85.8 4.7 %fusion.17 = bf16[1024,512]{1,0:T(8,128)(2,1)} fusion(bf16[1024,512]{1,0:T(8,128)(2,1)S(1)} %get-tuple-element.15, bf16[1024,4096]{1,0:T(8,128)(2,1)} %get-tuple-element.11.dense_ref), kind=kOutput, calls=%fused_computation.21 | convolution fusion | flops 1074266112 | bytes 4194304 | tf_op jit(solution)/shard_map/dot_general | solution.py:61
  91.2 1.7 collective-permute-start.4
  92.9 3.5 %collective-permute-start.6 = (bf16[1024,512]{1,0:T(8,128)(2,1)}, bf16[1024,512]{1,0:T(8,128)(2,1)}, u32[]{:S(2)}, u32[]{:S(2)}) collective-permute-start(bf16[1024,512]{1,0:T(8,128)(2,1)} %get-tuple-element.17), channel_id=1, source_target_pairs={{0,1},{3,2},{4,5},{7,6},{8,9},{11,10},{12,13},{15,14},{16,17},{19,... | collective-permute-start | bytes 3145736 | tf_op jit(solution)/shard_map/ppermute | solution.py:157
  99.6 3.9 %all-to-all-start.1 = ((bf16[8,192,512]{2,1,0:T(8,128)(2,1)}), bf16[8,192,512]{2,1,0:T(8,128)(2,1)S(1)}, u32[]{:S(2)}, u32[]{:S(2)}) async-start(bf16[8,192,512]{2,1,0:T(8,128)(2,1)} %pad_maximum_fusion), calls=%async_computation.1 | async-start | bytes 3145728 | tf_op jit(solution)/shard_map/all_to_all | solution.py:213
  103.5 3.0 %fusion.5 = f32[1024,512]{1,0:T(8,128)S(1)} fusion(bf16[1024,512]{1,0:T(8,128)(2,1)S(1)} %copy-done.6, bf16[1024,4096]{1,0:T(8,128)(2,1)} %get-tuple-element.11.dense_ref), kind=kOutput, calls=%fused_computation.8 | convolution fusion | flops 1073741824 | bytes 5242880 | tf_op jit(solution)/shard_map/dot_general | solution.py:61
  106.5 2.1 %fusion.38 = f32[1024,512]{1,0:T(8,128)} fusion(bf16[1024,512]{1,0:T(8,128)(2,1)S(1)} %copy-done.3, bf16[512,512]{1,0:T(8,128)(2,1)S(1)} %copy-done), kind=kOutput, calls=%fused_computation.49 | convolution fusion | flops 536870912 | bytes 3670016 | tf_op jit(solution)/shard_map/dot_general | solution.py:57
  108.6 4.3 %fusion.13 = f32[1024,512]{1,0:T(8,128)} fusion(bf16[1024,512]{1,0:T(8,128)(2,1)S(1)} %copy-done.6, bf16[1024,4096]{1,0:T(8,128)(2,1)} %get-tuple-element.11.dense_ref), kind=kOutput, calls=%fused_computation.16 | convolution fusion | flops 1073741824 | bytes 5242880 | tf_op jit(solution)/shard_map/dot_general | solution.py:61
  112.8 6.4 %collective-permute-done.6 = bf16[1024,512]{1,0:T(8,128)(2,1)} collective-permute-done((bf16[1024,512]{1,0:T(8,128)(2,1)}, bf16[1024,512]{1,0:T(8,128)(2,1)}, u32[]{:S(2)}, u32[]{:S(2)}) %collective-permute-start.6) | collective-permute-done | bytes 1048608 | tf_op jit(solution)/shard_map/ppermute | solution.py:157
  120.8 3.7 %all-to-all-done.1 = bf16[8,192,512]{2,1,0:T(8,128)(2,1)S(1)} async-done(((bf16[8,192,512]{2,1,0:T(8,128)(2,1)}), bf16[8,192,512]{2,1,0:T(8,128)(2,1)S(1)}, u32[]{:S(2)}, u32[]{:S(2)}) %all-to-all-start.1) | async-done | bytes 1572896 | tf_op jit(solution)/shard_map/all_to_all | solution.py:213
  125.3 3.9 %all-to-all-start.2 = ((f32[4,2,16,512]{3,2,1,0:T(8,128)}), f32[4,2,16,512]{3,2,1,0:T(8,128)S(1)}, u32[]{:S(2)}, u32[]{:S(2)}) async-start(f32[4,2,16,512]{3,2,1,0:T(8,128)} %bitcast.10), calls=%async_computation.2 | async-start | bytes 524288 | tf_op jit(solution)/shard_map/all_to_all | solution.py:217
  130.4 2.9 %collective-permute-start.7 = (bf16[512,512]{1,0:T(8,128)(2,1)}, bf16[512,512]{1,0:T(8,128)(2,1)}, u32[]{:S(2)}, u32[]{:S(2)}) collective-permute-start(bf16[512,512]{1,0:T(8,128)(2,1)} %get-tuple-element.20), channel_id=1, source_target_pairs={{0,2},{1,3},{2,0},{3,1},{4,6},{5,7},{6,4},{7,5},{8,10},{9,11},{10,... | collective-permute-start | bytes 1572872 | tf_op jit(solution)/shard_map/ppermute | solution.py:157
  133.4 2.3 %fusion.1 = f32[1024,512]{1,0:T(8,128)} fusion(bf16[512,512]{1,0:T(8,128)(2,1)S(1)} %bitcast.40, s32[512]{0:T(512)S(1)} %eq.17, pred[512]{0:T(512)(128)(4,1)S(1)} %lt.33), kind=kOutput, calls=%fused_computation.6 | convolution fusion | flops 537919488 | bytes 2624000 | tf_op jit(solution)/shard_map/dot_general | solution.py:61
  135.6 10.3 %all-to-all-done.2 = f32[4,2,16,512]{3,2,1,0:T(8,128)S(1)} async-done(((f32[4,2,16,512]{3,2,1,0:T(8,128)}), f32[4,2,16,512]{3,2,1,0:T(8,128)S(1)}, u32[]{:S(2)}, u32[]{:S(2)}) %all-to-all-start.2) | async-done | bytes 262176 | tf_op jit(solution)/shard_map/all_to_all | solution.py:217
  146.8 3.7 %all-to-all-start.3 = ((f32[8,2,16,512]{3,2,1,0:T(8,128)}), f32[8,2,16,512]{3,2,1,0:T(8,128)S(1)}, u32[]{:S(2)}, u32[]{:S(2)}) async-start(f32[8,2,16,512]{3,2,1,0:T(8,128)} %broadcast_in_dim.2), calls=%async_computation.3 | async-start | bytes 1048576 | tf_op jit(solution)/shard_map/all_to_all | solution.py:219
  150.6 3.8 %convert_add_fusion = f32[1024,512]{1,0:T(8,128)S(1)} fusion(bf16[1024,512]{1,0:T(8,128)(2,1)} %collective-permute-done.5, bf16[1024,512]{1,0:T(8,128)(2,1)} %collective-permute-done.4, f32[1024,512]{1,0:T(8,128)} %fusion.1, f32[1024,512]{1,0:T(8,128)S(1)} %copy-done.7, f32[1024,512]{1,0:T(8,128)} %fusion.13), kind=kLoop, calls=%fused_computation.2 | loop fusion | flops 3145728 | bytes 10485760 | tf_op jit(solution)/shard_map/add | solution.py:239
  154.4 19.0 %collective-permute-done.7 = bf16[512,512]{1,0:T(8,128)(2,1)} collective-permute-done((bf16[512,512]{1,0:T(8,128)(2,1)}, bf16[512,512]{1,0:T(8,128)(2,1)}, u32[]{:S(2)}, u32[]{:S(2)}) %collective-permute-start.7) | collective-permute-done | bytes 524320 | tf_op jit(solution)/shard_map/ppermute | solution.py:157
  173.4 7.1 %collective-permute-done.8 = bf16[512,512]{1,0:T(8,128)(2,1)} collective-permute-done((bf16[512,512]{1,0:T(8,128)(2,1)}, bf16[512,512]{1,0:T(8,128)(2,1)}, u32[]{:S(2)}, u32[]{:S(2)}) %collective-permute-start.8) | collective-permute-done | bytes 524320 | tf_op jit(solution)/shard_map/ppermute | solution.py:157
  180.4 1.6 fusion.28
  (52 shorter events, 13.8 us)
Async XLA Ops:
  0.6 15.4 %copy-start = (bf16[512,512]{1,0:T(8,128)(2,1)S(1)}, bf16[512,512]{1,0:T(8,128)(2,1)}, u32[]{:S(2)}) copy-start(bf16[512,512]{1,0:T(8,128)(2,1)} %param.13) | copy-start | bytes 1572868
  0.6 56.1 %collective-permute-start = (bf16[1024,512]{1,0:T(8,128)(2,1)}, bf16[1024,512]{1,0:T(8,128)(2,1)}, u32[]{:S(2)}, u32[]{:S(2)}) collective-permute-start(bf16[1024,512]{1,0:T(8,128)(2,1)} %param.12), channel_id=1, source_target_pairs={{0,1},{1,0},{2,3},{3,2},{4,5},{5,4},{6,7},{7,6},{8,9},{9,8},{10,11... | collective-permute-start | bytes 3145736 | tf_op jit(solution)/shard_map/ppermute | solution.py:157
  3.8 49.7 %collective-permute-start.1 = (bf16[1024,512]{1,0:T(8,128)(2,1)}, bf16[1024,512]{1,0:T(8,128)(2,1)}, u32[]{:S(2)}, u32[]{:S(2)}) collective-permute-start(bf16[1024,512]{1,0:T(8,128)(2,1)} %param.12), channel_id=1, source_target_pairs={{0,2},{1,3},{2,0},{3,1},{4,6},{5,7},{6,4},{7,5},{8,10},{9,11},{10,... | collective-permute-start | bytes 3145736 | tf_op jit(solution)/shard_map/ppermute | solution.py:157
  6.4 56.9 %collective-permute-start.3 = (bf16[1024,512]{1,0:T(8,128)(2,1)}, bf16[1024,512]{1,0:T(8,128)(2,1)}, u32[]{:S(2)}, u32[]{:S(2)}) collective-permute-start(bf16[1024,512]{1,0:T(8,128)(2,1)} %param.12), channel_id=1, source_target_pairs={{1,2},{2,1},{5,6},{6,5},{9,10},{10,9},{13,14},{14,13},{17,18},{18,... | collective-permute-start | bytes 3145736 | tf_op jit(solution)/shard_map/ppermute | solution.py:157
  12.3 42.4 %all-to-all-start = ((bf16[8,64,512]{2,1,0:T(8,128)(2,1)}), bf16[8,64,512]{2,1,0:T(8,128)(2,1)S(1)}, u32[]{:S(2)}, u32[]{:S(2)}) async-start(bf16[8,64,512]{2,1,0:T(8,128)(2,1)} %bitcast.1), calls=%async_computation | async-start | bytes 1048576 | tf_op jit(solution)/shard_map/all_to_all | solution.py:189
  16.1 2.0 %copy-start.11 = (s32[128]{0:T(128)S(1)}, s32[128]{0:T(128)}, u32[]{:S(2)}) copy-start(s32[128]{0:T(128)} %param.17) | copy-start | bytes 1540
  53.5 22.9 %collective-permute-start.2 = (bf16[1024,512]{1,0:T(8,128)(2,1)}, bf16[1024,512]{1,0:T(8,128)(2,1)}, u32[]{:S(2)}, u32[]{:S(2)}) collective-permute-start(bf16[1024,512]{1,0:T(8,128)(2,1)} %collective-permute-done.1), channel_id=1, source_target_pairs={{1,0},{2,3},{5,4},{6,7},{9,8},{10,11},{13,12},{14,15},{17,16},{18,... | collective-permute-start | bytes 3145736 | tf_op jit(solution)/shard_map/ppermute | solution.py:157
  56.7 3.3 %copy-start.8 = (f32[1024,512]{1,0:T(8,128)S(1)}, f32[1024,512]{1,0:T(8,128)}, u32[]{:S(2)}) copy-start(f32[1024,512]{1,0:T(8,128)} %fusion.15) | copy-start | bytes 6291460
  60.0 16.4 %copy-start.1 = (bf16[1024,512]{1,0:T(8,128)(2,1)S(1)}, bf16[1024,512]{1,0:T(8,128)(2,1)}, u32[]{:S(2)}) copy-start(bf16[1024,512]{1,0:T(8,128)(2,1)} %cot_ref.1) | copy-start | bytes 3145732
  60.0 16.4 %copy-start.4 = (bf16[512,512]{1,0:T(8,128)(2,1)S(1)}, bf16[512,512]{1,0:T(8,128)(2,1)}, u32[]{:S(2)}) copy-start(bf16[512,512]{1,0:T(8,128)(2,1)} %w_ref.1) | copy-start | bytes 1572868
  85.8 4.7 %copy-start.5 = (bf16[1024,512]{1,0:T(8,128)(2,1)}, bf16[1024,512]{1,0:T(8,128)(2,1)S(1)}, u32[]{:S(2)}) copy-start(bf16[1024,512]{1,0:T(8,128)(2,1)S(1)} %get-tuple-element.15) | copy-start | bytes 3145732
  85.8 11.4 %copy-start.2 = (bf16[1024,512]{1,0:T(8,128)(2,1)}, bf16[1024,512]{1,0:T(8,128)(2,1)S(1)}, u32[]{:S(2)}) copy-start(bf16[1024,512]{1,0:T(8,128)(2,1)S(1)} %get-tuple-element.14) | copy-start | bytes 3145732
  85.8 4.7 %copy-start.10 = (bf16[1024,512]{1,0:T(8,128)(2,1)S(1)}, bf16[1024,512]{1,0:T(8,128)(2,1)}, u32[]{:S(2)}) copy-start(bf16[1024,512]{1,0:T(8,128)(2,1)} %get-tuple-element.12) | copy-start | bytes 3145732
  90.4 5.9 %copy-start.9 = (bf16[1024,512]{1,0:T(8,128)(2,1)S(1)}, bf16[1024,512]{1,0:T(8,128)(2,1)}, u32[]{:S(2)}) copy-start(bf16[1024,512]{1,0:T(8,128)(2,1)} %param.12) | copy-start | bytes 3145732
  91.2 59.4 %collective-permute-start.4 = (bf16[1024,512]{1,0:T(8,128)(2,1)}, bf16[1024,512]{1,0:T(8,128)(2,1)}, u32[]{:S(2)}, u32[]{:S(2)}) collective-permute-start(bf16[1024,512]{1,0:T(8,128)(2,1)} %get-tuple-element.17), channel_id=1, source_target_pairs={{1,2},{2,1},{5,6},{6,5},{9,10},{10,9},{13,14},{14,13},{17,18},{18,... | collective-permute-start | bytes 3145736 | tf_op jit(solution)/shard_map/ppermute | solution.py:157
  92.9 26.3 %collective-permute-start.6 = (bf16[1024,512]{1,0:T(8,128)(2,1)}, bf16[1024,512]{1,0:T(8,128)(2,1)}, u32[]{:S(2)}, u32[]{:S(2)}) collective-permute-start(bf16[1024,512]{1,0:T(8,128)(2,1)} %get-tuple-element.17), channel_id=1, source_target_pairs={{0,1},{3,2},{4,5},{7,6},{8,9},{11,10},{12,13},{15,14},{16,17},{19,... | collective-permute-start | bytes 3145736 | tf_op jit(solution)/shard_map/ppermute | solution.py:157
  96.3 54.2 %collective-permute-start.5 = (bf16[1024,512]{1,0:T(8,128)(2,1)}, bf16[1024,512]{1,0:T(8,128)(2,1)}, u32[]{:S(2)}, u32[]{:S(2)}) collective-permute-start(bf16[1024,512]{1,0:T(8,128)(2,1)} %fusion.17), channel_id=1, source_target_pairs={{0,1},{1,0},{2,3},{3,2},{4,5},{5,4},{6,7},{7,6},{8,9},{9,8},{10,11... | collective-permute-start | bytes 3145736 | tf_op jit(solution)/shard_map/ppermute | solution.py:157
  99.6 3.9 %copy-start.6 = (bf16[1024,512]{1,0:T(8,128)(2,1)S(1)}, bf16[1024,512]{1,0:T(8,128)(2,1)}, u32[]{:S(2)}) copy-start(bf16[1024,512]{1,0:T(8,128)(2,1)} %copy-done.5) | copy-start | bytes 3145732
  99.6 24.9 %all-to-all-start.1 = ((bf16[8,192,512]{2,1,0:T(8,128)(2,1)}), bf16[8,192,512]{2,1,0:T(8,128)(2,1)S(1)}, u32[]{:S(2)}, u32[]{:S(2)}) async-start(bf16[8,192,512]{2,1,0:T(8,128)(2,1)} %pad_maximum_fusion), calls=%async_computation.1 | async-start | bytes 3145728 | tf_op jit(solution)/shard_map/all_to_all | solution.py:213
  103.5 3.0 %copy-start.3 = (bf16[1024,512]{1,0:T(8,128)(2,1)S(1)}, bf16[1024,512]{1,0:T(8,128)(2,1)}, u32[]{:S(2)}) copy-start(bf16[1024,512]{1,0:T(8,128)(2,1)} %copy-done.2) | copy-start | bytes 3145732
  125.3 20.6 %all-to-all-start.2 = ((f32[4,2,16,512]{3,2,1,0:T(8,128)}), f32[4,2,16,512]{3,2,1,0:T(8,128)S(1)}, u32[]{:S(2)}, u32[]{:S(2)}) async-start(f32[4,2,16,512]{3,2,1,0:T(8,128)} %bitcast.10), calls=%async_computation.2 | async-start | bytes 524288 | tf_op jit(solution)/shard_map/all_to_all | solution.py:217
  130.4 43.0 %collective-permute-start.7 = (bf16[512,512]{1,0:T(8,128)(2,1)}, bf16[512,512]{1,0:T(8,128)(2,1)}, u32[]{:S(2)}, u32[]{:S(2)}) collective-permute-start(bf16[512,512]{1,0:T(8,128)(2,1)} %get-tuple-element.20), channel_id=1, source_target_pairs={{0,2},{1,3},{2,0},{3,1},{4,6},{5,7},{6,4},{7,5},{8,10},{9,11},{10,... | collective-permute-start | bytes 1572872 | tf_op jit(solution)/shard_map/ppermute | solution.py:157
  133.3 47.2 %collective-permute-start.8 = (bf16[512,512]{1,0:T(8,128)(2,1)}, bf16[512,512]{1,0:T(8,128)(2,1)}, u32[]{:S(2)}, u32[]{:S(2)}) collective-permute-start(bf16[512,512]{1,0:T(8,128)(2,1)} %get-tuple-element.21), channel_id=1, source_target_pairs={{0,2},{1,3},{2,0},{3,1},{4,6},{5,7},{6,4},{7,5},{8,10},{9,11},{10,... | collective-permute-start | bytes 1572872 | tf_op jit(solution)/shard_map/ppermute | solution.py:157
  133.3 17.2 %copy-start.7 = (f32[1024,512]{1,0:T(8,128)S(1)}, f32[1024,512]{1,0:T(8,128)}, u32[]{:S(2)}) copy-start(f32[1024,512]{1,0:T(8,128)} %fusion.38) | copy-start | bytes 6291460
  146.8 36.3 %all-to-all-start.3 = ((f32[8,2,16,512]{3,2,1,0:T(8,128)}), f32[8,2,16,512]{3,2,1,0:T(8,128)S(1)}, u32[]{:S(2)}, u32[]{:S(2)}) async-start(f32[8,2,16,512]{3,2,1,0:T(8,128)} %broadcast_in_dim.2), calls=%async_computation.3 | async-start | bytes 1048576 | tf_op jit(solution)/shard_map/all_to_all | solution.py:219
where the time goes:
time: 185 us; the launch traced here: 184 us
  waiting for transfers between devices  77.3 us (42%)
  matrix products  36.1 us (20%)
  starting transfers between devices  32 us (17%)
  Pallas kernels  22 us (12%)
  other arithmetic  11.6 us (6%)
  local copies, waits for them, and re-layouts  4.04 us (2%)
    ppermute x9, waiting for transfers between devices, move(): return lax.ppermute(value, 'rep', pairs)  63.3 us
    dot_general x7, matrix products, dot(): return jnp.dot(a, b, preferred_element_type=jnp.float32)  19.7 us
    ppermute x9, starting transfers between devices, move(): return lax.ppermute(value, 'rep', pairs)  16.7 us
    dot_general x7, matrix products, dot_t(): lax.dot_general(a, b, (((0,), (0,)), ((), ())), preferred_element_type=jn...  16.4 us
    pallas_call x1, Pallas kernels, densify(): pl.pallas_call(densify_kernel, out_shape=(jax.ShapeDtypeStruct((rows, col...  12.7 us
    all_to_all x1, waiting for transfers between devices, per_device(): both = lax.all_to_all(both, 'rep', split_axis=0, concat_axis=0, tiled=True)  10.3 us
    pallas_call x1, Pallas kernels, middle(): pl.pallas_call(middle_kernel, grid=(rows // step,), out_shape=(like,) * 5...  9.36 us
    all_to_all x1, starting transfers between devices, per_device(): both = lax.all_to_all(both, 'rep', split_axis=0, concat_axis=0, tiled=True)  3.94 us
  transfers between devices with their start and end apart: 13, of which 7 were waited for; matrix products, arithmetic and copies ran while one was open for 25% of the time, Pallas kernels for 7%

commit v1 on v0

--- a/solution.py
+++ b/solution.py
@@ -66,13 +66,14 @@
     out_ref, neighbour_ref, grad_ref, agg_ref, term_ref, total, far,
 ):
     step = pl.program_id(0)
+    half = far.shape[0]
 
     @pl.when(step == 0)
     def _():
         far[...] = outer_ref[...] + inner_ref[...]
 
     dense = dense_ref[...]
-    neighbour = (acc_ref[...] + dot(dense, far[...])).astype(jnp.bfloat16)
+    neighbour = (acc_ref[...] + dot(dense[:, -half:], far[...])).astype(jnp.bfloat16)
     neighbour_ref[...] = neighbour
     preact = pre_ref[...] + dot(neighbour, w_ref[...])
     sigmoid_pre = jax.nn.sigmoid(preact)
@@ -111,14 +112,14 @@
         in_specs=[
             by_rows,
             pl.BlockSpec((step, rows), lambda i: (i, slot)),
-            pl.BlockSpec((rows, width), lambda i: (0, 0)),
-            pl.BlockSpec((rows, width), lambda i: (0, 0)),
+            pl.BlockSpec(outer.shape, lambda i: (0, 0)),
+            pl.BlockSpec(outer.shape, lambda i: (0, 0)),
             by_rows,
             by_rows,
             pl.BlockSpec(w_neigh.shape, lambda i: (0, 0)),
         ],
         out_specs=(by_rows,) * 4 + (pl.BlockSpec((rows, width), lambda i: (0, 0)),),
-        scratch_shapes=[pltpu.VMEM((rows, width), jnp.float32), pltpu.VMEM((rows, width), jnp.bfloat16)],
+        scratch_shapes=[pltpu.VMEM((rows, width), jnp.float32), pltpu.VMEM(outer.shape, jnp.bfloat16)],
         compiler_params=pltpu.CompilerParams(vmem_limit_bytes=40 << 20),
         cost_estimate=pl.CostEstimate(
             flops=4 * rows * width * (rows + width), bytes_accessed=18 << 20, transcendentals=rows * width
@@ -148,19 +149,26 @@
     me = lax.axis_index("rep")
     blocks = row_count // tile_size
     assert n == 4
-    swap_one = [(0, 1), (1, 0), (2, 3), (3, 2)]
-    swap_two = [(0, 2), (1, 3), (2, 0), (3, 1)]
+    first_out = [(0, 1), (3, 2), (1, 3), (2, 0)]
+    second_out = [(0, 2), (3, 1), (1, 0), (2, 3)]
+    first_in = [(b, a) for a, b in first_out]
+    second_in = [(b, a) for a, b in second_out]
     swap_inner = [(1, 2), (2, 1)]
     outward, inward = [(1, 0), (2, 3)], [(0, 1), (3, 2)]
 
     def move(value, pairs):
         return lax.ppermute(value, "rep", pairs)
 
-    second = move(features, swap_two)
-    first = move(features, swap_one)
-    inner = move(features, swap_inner)
+    half = row_count // 2
+    low, high = features[:half], features[half:]
+    second = move(features, second_in)
+    first_a = move(low, first_in)
+    first_b = move(high, first_in)
+    inner_a, inner_b = move(low, swap_inner), move(high, swap_inner)
 
     slot = jnp.bitwise_xor(local_cols // blocks, me)
+    crossed = ((me == 1) | (me == 2)) & ((slot == 1) | (slot == 2))
+    slot = jnp.where(crossed, 3 - slot, slot)
     slot_cols = slot * blocks + local_cols % blocks
     cut_list = cut_rows[0, 0]
     halo_size = cut_list.shape[0] * cut_list.shape[1]
@@ -192,11 +200,14 @@
 
     pre_self = dot(features, w_self)
     summed = dot(part(0), features) + dot(hdense, incoming)
-    third = move(second, outward)
-    summed = summed + dot(part(1), first)
+    third_a = move(first_a, outward)
+    third_b = move(first_b, outward)
     summed = summed + dot(part(2), second)
+    summed = summed + dot(part(1)[:, :half], first_a) + dot(part(1)[:, half:], first_b)
+    summed = lax.optimization_barrier(summed)
+    summed = summed + dot(part(3)[:, :half], third_a + inner_a)
     out, neighbour, grad_pre, grad_agg, term = middle(
-        summed, dense, 3, third, inner, pre_self, cotangent, w_neigh
+        summed, dense, 3, third_b, inner_b, pre_self, cotangent, w_neigh
     )
 
     passed = move(term, inward)
@@ -216,8 +227,9 @@
     both = jnp.sum(both[:, slots:].astype(jnp.float32), axis=0).reshape(n, 2, share, width)
     both = lax.all_to_all(both, "rep", split_axis=0, concat_axis=0, tiled=True)
     both = jnp.sum(both, axis=0)
+    both = jnp.broadcast_to(both[None], (dom, 2, share, width))
     both = lax.all_to_all(
-        jnp.broadcast_to(both[None], (dom, 2, share, width)),
+        both,
         "dom",
         split_axis=0,
         concat_axis=0,
@@ -226,24 +238,22 @@
     d_w_self = both[:, 0].reshape(width // n, width)
     d_w_neigh = both[:, 1].reshape(width // n, width)
 
-    one_term = dot_t(part(1), grad_agg).astype(jnp.bfloat16)
-    one = move(one_term, swap_one)
-    two_term = lax.optimization_barrier(dot_t(part(2), grad_agg))
-    two_term = (two_term + passed.astype(jnp.float32)).astype(jnp.bfloat16)
-    half = row_count // 2
-    two_a = move(two_term[:half], swap_two)
-    two_b = move(two_term[half:], swap_two)
+    second_term = dot_t(part(2), grad_agg).astype(jnp.bfloat16)
+    second_back = move(second_term, second_out)
+    first_term = lax.optimization_barrier(dot_t(part(1), grad_agg))
+    first_term = first_term + passed.astype(jnp.float32)
+    last_a = move(first_term[:half].astype(jnp.bfloat16), first_out)
+    last_b = move(first_term[half:].astype(jnp.bfloat16), first_out)
 
     d_x = dot(grad_pre, w_self.T) + dot_t(part(0), grad_agg)
     d_x = d_x + dot_t(selector, returned)
-    d_x = d_x + near.astype(jnp.float32) + one.astype(jnp.float32)
+    d_x = d_x + near.astype(jnp.float32)
+    d_x = d_x + second_back.astype(jnp.float32)
     d_x = lax.optimization_barrier(d_x)
-    d_x = jnp.concatenate(
-        [
-            (d_x[:half] + two_a.astype(jnp.float32)).astype(jnp.bfloat16),
-            (d_x[half:] + two_b.astype(jnp.float32)).astype(jnp.bfloat16),
-        ]
-    )
+    base = jnp.concatenate([last_a.astype(jnp.float32), jnp.zeros((row_count - half, width))])
+    base = lax.optimization_barrier((d_x + base).astype(jnp.bfloat16))
+    last = (d_x[half:] + last_b.astype(jnp.float32)).astype(jnp.bfloat16)
+    d_x = lax.dynamic_update_slice_in_dim(base, last, half, 0)
     return (out, d_x, d_w_self, d_w_neigh)
 
 

time: 185 us -> 193 us (1.043)
  starting transfers between devices: 32 us -> 38 us
    ppermute x9 -> x12, waiting for transfers between devices: 63.3 us -> 35 us  [move(): return lax.ppermute(value, 'rep', pairs)]
    all_to_all x1, waiting for transfers between devices: 10.3 us -> 37.2 us  [per_device(): both = lax.all_to_all(both, 'rep', split_axis=0, concat_axis=0, tiled=True)]
    ppermute x9 -> x12, starting transfers between devices: 16.7 us -> 22.5 us  [move(): return lax.ppermute(value, 'rep', pairs)]
    all_to_all x1 -> x2, starting transfers between devices: 3.86 us -> 7.66 us  [per_device(): both = lax.all_to_all(both, 'dom', split_axis=0, concat_axis=0, tiled=True)]
    all_to_all x1 -> x0, starting transfers between devices: 3.73 us -> none  [per_device(): lax.all_to_all(jnp.broadcast_to(both[None], (dom, 2, share, width)), 'dom...]
    slice x1 -> x2, local copies, waits for them, and re-layouts: 1.09 us -> 3.3 us  [the longest x1 2.23 us: per_device(): low, high = (features[:half], features[half:])]
    dynamic_update_slice x0 -> x1, other arithmetic: none -> 2 us  [per_device(): d_x = lax.dynamic_update_slice_in_dim(base, last, half, 0)]
    all_to_all x1 -> x2, waiting for transfers between devices: 3.68 us -> 5.47 us  [per_device(): both = lax.all_to_all(both, 'dom', split_axis=0, concat_axis=0, tiled=True)]
  transfers between devices with their start and end apart: 13 -> 16, of which waited for: 7 -> 8; matrix products, arithmetic and copies ran while one was open for 25% -> 26% of each run, Pallas kernels for 7% -> 7%
where the time goes in v1:
time: 193 us; the launch traced here: 192 us
  waiting for transfers between devices  77.7 us (40%)
  starting transfers between devices  38 us (20%)
  matrix products  36 us (19%)
  Pallas kernels  20.8 us (11%)
  other arithmetic  13.1 us (7%)
  local copies, waits for them, and re-layouts  5.79 us (3%)
    all_to_all x1, waiting for transfers between devices, per_device(): both = lax.all_to_all(both, 'rep', split_axis=0, concat_axis=0, tiled=True)  37.2 us
    ppermute x12, waiting for transfers between devices, move(): return lax.ppermute(value, 'rep', pairs)  35 us
    ppermute x12, starting transfers between devices, move(): return lax.ppermute(value, 'rep', pairs)  22.5 us
    dot_general x9, matrix products, dot(): return jnp.dot(a, b, preferred_element_type=jnp.float32)  20.4 us
    dot_general x7, matrix products, dot_t(): lax.dot_general(a, b, (((0,), (0,)), ((), ())), preferred_element_type=jn...  15.6 us
    pallas_call x1, Pallas kernels, densify(): pl.pallas_call(densify_kernel, out_shape=(jax.ShapeDtypeStruct((rows, col...  12.7 us
    pallas_call x1, Pallas kernels, middle(): pl.pallas_call(middle_kernel, grid=(rows // step,), out_shape=(like,) * 5...  8.13 us
    all_to_all x2, starting transfers between devices, per_device(): both = lax.all_to_all(both, 'dom', split_axis=0, concat_axis=0, tiled=True)  7.66 us
  transfers between devices with their start and end apart: 16, of which 8 were waited for; matrix products, arithmetic and copies ran while one was open for 26% of the time, Pallas kernels for 7%

profile of v1, /device:TPU:0, one launch (start us, length us, event | category | flops | bytes accessed | tf_op | source)
XLA Modules:
  0.0 192.3 jit_solution(1435294771954497749)
XLA Ops:
  0.7 3.1 %collective-permute-start = (bf16[1024,512]{1,0:T(8,128)(2,1)}, bf16[1024,512]{1,0:T(8,128)(2,1)}, u32[]{:S(2)}, u32[]{:S(2)}) collective-permute-start(bf16[1024,512]{1,0:T(8,128)(2,1)} %param.12), channel_id=1, source_target_pairs={{2,0},{1,3},{0,1},{3,2},{6,4},{5,7},{4,5},{7,6},{10,8},{9,11},{8,9... | collective-permute-start | bytes 3145736 | tf_op jit(solution)/shard_map/ppermute | solution.py:160
  3.8 2.2 %fusion.39 = (bf16[512,512]{1,0:T(8,128)(2,1)}, bf16[512,512]{1,0:T(8,128)(2,1)}) fusion(bf16[1024,512]{1,0:T(8,128)(2,1)} %param.12), kind=kLoop, calls=%fused_computation.51 | loop fusion | bytes 2097152 | tf_op jit(solution)/shard_map/slice | solution.py:163
  8.6 3.4 %collective-permute-start.2 = (bf16[512,512]{1,0:T(8,128)(2,1)}, bf16[512,512]{1,0:T(8,128)(2,1)}, u32[]{:S(2)}, u32[]{:S(2)}) collective-permute-start(bf16[512,512]{1,0:T(8,128)(2,1)} %get-tuple-element.20), channel_id=1, source_target_pairs={{1,0},{2,3},{3,1},{0,2},{5,4},{6,7},{7,5},{4,6},{9,8},{10,11},{11,... | collective-permute-start | bytes 1572872 | tf_op jit(solution)/shard_map/ppermute | solution.py:160
  14.5 4.1 %all-to-all-start = ((bf16[8,64,512]{2,1,0:T(8,128)(2,1)}), bf16[8,64,512]{2,1,0:T(8,128)(2,1)}, u32[]{:S(2)}, u32[]{:S(2)}) async-start(bf16[8,64,512]{2,1,0:T(8,128)(2,1)} %bitcast.1), calls=%async_computation | async-start | bytes 1048576 | tf_op jit(solution)/shard_map/all_to_all | solution.py:197
  19.3 12.7 %densify.1 = (bf16[1024,4096]{1,0:T(8,128)(2,1)}, bf16[1024,512]{1,0:T(8,128)(2,1)}) custom-call(s32[128]{0:T(128)} %local_rows.1, s32[128]{0:T(128)} %fusion.37.local_cols, s32[96]{0:T(128)} %halo_rows.1, s32[96]{0:T(128)} %halo_cols.1, bf16[128,128,128]{2,1,0:T(8,128)(2,1)} %local_ref.1, bf16[96,128,128]{2,1,0:T(8,128)(2,1)} %halo_ref.1), custom_call_target="tpu_custom_call" | custom-call | flops 8388608 | bytes 18874368 | tf_op jit(solution)/shard_map/densify/pallas_call | solution.py:39
  31.9 4.3 %fusion.13 = f32[1024,512]{1,0:T(8,128)} fusion(bf16[1024,512]{1,0:T(8,128)(2,1)S(1)} %copy-done.7, bf16[1024,4096]{1,0:T(8,128)(2,1)} %get-tuple-element.11.dense_ref), kind=kOutput, calls=%fused_computation.17 | convolution fusion | flops 1073741824 | bytes 5242880 | tf_op jit(solution)/shard_map/dot_general | solution.py:57
  37.0 2.1 %fusion.41 = f32[1024,512]{1,0:T(8,128)S(1)} fusion(bf16[1024,512]{1,0:T(8,128)(2,1)} %get-tuple-element.12, bf16[512,512]{1,0:T(8,128)(2,1)} %bitcast.2), kind=kOutput, calls=%fused_computation.53 | convolution fusion | flops 536870912 | bytes 3670016 | tf_op jit(solution)/shard_map/dot_general | solution.py:57
  40.9 9.9 %collective-permute-done.2 = bf16[512,512]{1,0:T(8,128)(2,1)} collective-permute-done((bf16[512,512]{1,0:T(8,128)(2,1)}, bf16[512,512]{1,0:T(8,128)(2,1)}, u32[]{:S(2)}, u32[]{:S(2)}) %collective-permute-start.2) | collective-permute-done | bytes 524320 | tf_op jit(solution)/shard_map/ppermute | solution.py:160
  52.1 2.1 %fusion.29 = f32[1024,512]{1,0:T(8,128)S(1)} fusion(bf16[512,512]{1,0:T(8,128)(2,1)} %collective-permute-done.1, bf16[1024,4096]{1,0:T(8,128)(2,1)} %get-tuple-element.11.dense_ref), kind=kOutput, calls=%fused_computation.34 | convolution fusion | flops 536870912 | bytes 3670016 | tf_op jit(solution)/shard_map/dot_general | solution.py:57
  54.2 3.3 %fusion.9 = f32[1024,512]{1,0:T(8,128)S(1)} fusion(bf16[1024,512]{1,0:T(8,128)(2,1)} %collective-permute-done, bf16[1024,4096]{1,0:T(8,128)(2,1)} %get-tuple-element.11.dense_ref), kind=kOutput, calls=%fused_computation.13 | convolution fusion | flops 1073741824 | bytes 5242880 | tf_op jit(solution)/shard_map/dot_general | solution.py:57
  57.5 2.2 %add_add_fusion = f32[1024,512]{1,0:T(8,128)S(1)} fusion(f32[1024,512]{1,0:T(8,128)S(1)} %fusion.29, f32[1024,512]{1,0:T(8,128)S(1)} %fusion.9, f32[1024,512]{1,0:T(8,128)S(1)} %copy-done.10, f32[1024,512]{1,0:T(8,128)S(1)} %fusion.41, bf16[512,512]{1,0:T(8,128)(2,1)} %collective-permute-done.2, bf16[1024,4096]{1,0:T(8,128)(2,1)} %get-tuple-element.11.dense_ref), kind=kOutput, calls=%fused_computation.6 | convolution fusion | flops 538968064 | bytes 12058624 | tf_op jit(solution)/shard_map/dot_general | solution.py:57
  59.7 2.3 %collective-permute-done.3 = bf16[512,512]{1,0:T(8,128)(2,1)S(1)} collective-permute-done((bf16[512,512]{1,0:T(8,128)(2,1)}, bf16[512,512]{1,0:T(8,128)(2,1)S(1)}, u32[]{:S(2)}, u32[]{:S(2)}) %collective-permute-start.3) | collective-permute-done | bytes 524320 | tf_op jit(solution)/shard_map/ppermute | solution.py:160
  62.0 2.1 %convolution_add_fusion.acc_ref = f32[1024,512]{1,0:T(8,128)S(1)} fusion(f32[1024,512]{1,0:T(8,128)S(1)} %add_add_fusion, bf16[1024,4096]{1,0:T(8,128)(2,1)} %get-tuple-element.11.dense_ref, bf16[512,512]{1,0:T(8,128)(2,1)S(1)} %collective-permute-done.3, bf16[512,512]{1,0:T(8,128)(2,1)} %collective-permute-done.4), kind=kOutput, calls=%fused_computation.19 | convolution fusion | flops 537657344 | bytes 6291456 | tf_op jit(solution)/shard_map/dot_general | solution.py:57
  64.1 9.0 %collective-permute-done.5.outer_ref = bf16[512,512]{1,0:T(8,128)(2,1)S(1)} collective-permute-done((bf16[512,512]{1,0:T(8,128)(2,1)}, bf16[512,512]{1,0:T(8,128)(2,1)S(1)}, u32[]{:S(2)}, u32[]{:S(2)}) %collective-permute-start.5) | collective-permute-done | bytes 524320 | tf_op jit(solution)/shard_map/ppermute | solution.py:160
  73.1 8.1 %middle.1 = (bf16[1024,512]{1,0:T(8,128)(2,1)}, bf16[1024,512]{1,0:T(8,128)(2,1)S(1)}, bf16[1024,512]{1,0:T(8,128)(2,1)S(1)}, bf16[1024,512]{1,0:T(8,128)(2,1)S(1)}, bf16[1024,512]{1,0:T(8,128)(2,1)}) custom-call(f32[1024,512]{1,0:T(8,128)S(1)} %convolution_add_fusion.acc_ref, bf16[1024,4096]{1,0:T(8,128)(2,1)} %get-tuple-element.11.dense_ref, ...), custom_call_target="tpu_custom_call" | custom-call | flops 3221225472 | bytes 18874368 | tf_op jit(solution)/shard_map/middle/pallas_call | solution.py:108
  82.2 3.9 %fusion.15 = bf16[1024,512]{1,0:T(8,128)(2,1)} fusion(bf16[1024,512]{1,0:T(8,128)(2,1)S(1)} %get-tuple-element.15, bf16[1024,4096]{1,0:T(8,128)(2,1)} %get-tuple-element.11.dense_ref), kind=kOutput, calls=%fused_computation.21 | convolution fusion | flops 1074266112 | bytes 4194304 | tf_op jit(solution)/shard_map/dot_general | solution.py:61
  86.2 3.9 %collective-permute-start.9 = (bf16[1024,512]{1,0:T(8,128)(2,1)}, bf16[1024,512]{1,0:T(8,128)(2,1)}, u32[]{:S(2)}, u32[]{:S(2)}) collective-permute-start(bf16[1024,512]{1,0:T(8,128)(2,1)} %get-tuple-element.17), channel_id=1, source_target_pairs={{0,1},{3,2},{4,5},{7,6},{8,9},{11,10},{12,13},{15,14},{16,17},{19,... | collective-permute-start | bytes 3145736 | tf_op jit(solution)/shard_map/ppermute | solution.py:160
  93.3 3.9 %all-to-all-start.1 = ((bf16[8,192,512]{2,1,0:T(8,128)(2,1)}), bf16[8,192,512]{2,1,0:T(8,128)(2,1)S(1)}, u32[]{:S(2)}, u32[]{:S(2)}) async-start(bf16[8,192,512]{2,1,0:T(8,128)(2,1)} %pad_maximum_fusion), calls=%async_computation.1 | async-start | bytes 3145728 | tf_op jit(solution)/shard_map/all_to_all | solution.py:224
  97.2 3.0 %fusion = f32[1024,512]{1,0:T(8,128)S(1)} fusion(bf16[1024,512]{1,0:T(8,128)(2,1)S(1)} %copy-done.6, bf16[1024,4096]{1,0:T(8,128)(2,1)} %get-tuple-element.11.dense_ref), kind=kOutput, calls=%fused_computation.3 | convolution fusion | flops 1073741824 | bytes 5242880 | tf_op jit(solution)/shard_map/dot_general | solution.py:61
  102.5 2.1 %fusion.43 = f32[1024,512]{1,0:T(8,128)} fusion(bf16[1024,512]{1,0:T(8,128)(2,1)S(1)} %copy-done.2, bf16[512,512]{1,0:T(8,128)(2,1)S(1)} %copy-done), kind=kOutput, calls=%fused_computation.55 | convolution fusion | flops 536870912 | bytes 3670016 | tf_op jit(solution)/shard_map/dot_general | solution.py:57
  104.7 4.2 %fusion.11 = f32[1024,512]{1,0:T(8,128)} fusion(bf16[1024,512]{1,0:T(8,128)(2,1)S(1)} %copy-done.6, bf16[1024,4096]{1,0:T(8,128)(2,1)} %get-tuple-element.11.dense_ref), kind=kOutput, calls=%fused_computation.15 | convolution fusion | flops 1073741824 | bytes 5242880 | tf_op jit(solution)/shard_map/dot_general | solution.py:61
  108.9 4.0 %collective-permute-done.9 = bf16[1024,512]{1,0:T(8,128)(2,1)} collective-permute-done((bf16[1024,512]{1,0:T(8,128)(2,1)}, bf16[1024,512]{1,0:T(8,128)(2,1)}, u32[]{:S(2)}, u32[]{:S(2)}) %collective-permute-start.9) | collective-permute-done | bytes 1048608 | tf_op jit(solution)/shard_map/ppermute | solution.py:160
  115.6 2.5 %collective-permute-start.10 = (bf16[512,512]{1,0:T(8,128)(2,1)}, bf16[512,512]{1,0:T(8,128)(2,1)}, u32[]{:S(2)}, u32[]{:S(2)}) collective-permute-start(bf16[512,512]{1,0:T(8,128)(2,1)} %get-tuple-element.19), channel_id=1, source_target_pairs={{0,1},{3,2},{1,3},{2,0},{4,5},{7,6},{5,7},{6,4},{8,9},{11,10},{9,1... | collective-permute-start | bytes 1572872 | tf_op jit(solution)/shard_map/ppermute | solution.py:160
  119.4 2.3 %fusion.3 = f32[1024,512]{1,0:T(8,128)} fusion(bf16[512,512]{1,0:T(8,128)(2,1)S(1)} %bitcast.40, s32[512]{0:T(512)S(1)} %eq.38, pred[512]{0:T(512)(128)(4,1)S(1)} %lt.33), kind=kOutput, calls=%fused_computation.9 | convolution fusion | flops 537919488 | bytes 2624000 | tf_op jit(solution)/shard_map/dot_general | solution.py:61
  122.5 3.7 %all-to-all-start.2 = ((f32[4,2,16,512]{3,2,1,0:T(8,128)}), f32[4,2,16,512]{3,2,1,0:T(8,128)S(1)}, u32[]{:S(2)}, u32[]{:S(2)}) async-start(f32[4,2,16,512]{3,2,1,0:T(8,128)} %bitcast.10), calls=%async_computation.2 | async-start | bytes 524288 | tf_op jit(solution)/shard_map/all_to_all | solution.py:228
  126.3 9.1 %collective-permute-done.8 = bf16[1024,512]{1,0:T(8,128)(2,1)} collective-permute-done((bf16[1024,512]{1,0:T(8,128)(2,1)}, bf16[1024,512]{1,0:T(8,128)(2,1)}, u32[]{:S(2)}, u32[]{:S(2)}) %collective-permute-start.8) | collective-permute-done | bytes 1048608 | tf_op jit(solution)/shard_map/ppermute | solution.py:160
  135.4 4.4 %convert_add_fusion = f32[1024,512]{1,0:T(8,128)S(1)} fusion(bf16[1024,512]{1,0:T(8,128)(2,1)} %collective-permute-done.8, bf16[1024,512]{1,0:T(8,128)(2,1)} %collective-permute-done.7, f32[1024,512]{1,0:T(8,128)} %fusion.3, f32[1024,512]{1,0:T(8,128)} %fusion.43, f32[1024,512]{1,0:T(8,128)} %fusion.11), kind=kLoop, calls=%fused_computation.5 | loop fusion | flops 3145728 | bytes 10485760 | tf_op jit(solution)/shard_map/add | solution.py:251
  139.8 37.2 %all-to-all-done.2 = f32[4,2,16,512]{3,2,1,0:T(8,128)S(1)} async-done(((f32[4,2,16,512]{3,2,1,0:T(8,128)}), f32[4,2,16,512]{3,2,1,0:T(8,128)S(1)}, u32[]{:S(2)}, u32[]{:S(2)}) %all-to-all-start.2) | async-done | bytes 262176 | tf_op jit(solution)/shard_map/all_to_all | solution.py:228
  177.9 3.8 %all-to-all-start.3 = ((f32[8,2,16,512]{3,2,1,0:T(8,128)}), f32[8,2,16,512]{3,2,1,0:T(8,128)S(1)}, u32[]{:S(2)}, u32[]{:S(2)}) async-start(f32[8,2,16,512]{3,2,1,0:T(8,128)} %broadcast_in_dim.2), calls=%async_computation.3 | async-start | bytes 1048576 | tf_op jit(solution)/shard_map/all_to_all | solution.py:231
  181.7 2.2 %add_convert_fusion = bf16[1024,512]{1,0:T(8,128)(2,1)} fusion(f32[1024,512]{1,0:T(8,128)S(1)} %convert_add_fusion, bf16[512,512]{1,0:T(8,128)(2,1)} %collective-permute-done.10), kind=kLoop, calls=%fused_computation.1 | loop fusion | flops 1572864 | bytes 3670016 | tf_op jit(solution)/shard_map/convert_element_type | solution.py:254
  184.0 2.0 %fusion.35 = bf16[1024,512]{1,0:T(8,128)(2,1)} fusion(bf16[1024,512]{1,0:T(8,128)(2,1)} %add_convert_fusion, bf16[512,512]{1,0:T(8,128)(2,1)} %collective-permute-done.11, f32[1024,512]{1,0:T(8,128)S(1)} %convert_add_fusion), kind=kLoop, calls=%fused_computation.40 | loop fusion | flops 786432 | bytes 2097152 | tf_op jit(solution)/shard_map/dynamic_update_slice | solution.py:256
  186.0 5.5 %all-to-all-done.3 = f32[8,2,16,512]{3,2,1,0:T(8,128)S(1)} async-done(((f32[8,2,16,512]{3,2,1,0:T(8,128)}), f32[8,2,16,512]{3,2,1,0:T(8,128)S(1)}, u32[]{:S(2)}, u32[]{:S(2)}) %all-to-all-start.3) | async-done | bytes 524320 | tf_op jit(solution)/shard_map/all_to_all | solution.py:231
  (67 shorter events, 22.7 us)
Async XLA Ops:
  0.6 35.6 %copy-start = (bf16[512,512]{1,0:T(8,128)(2,1)S(1)}, bf16[512,512]{1,0:T(8,128)(2,1)}, u32[]{:S(2)}) copy-start(bf16[512,512]{1,0:T(8,128)(2,1)} %param.13) | copy-start | bytes 1572868
  0.6 12.3 %copy-start.7 = (bf16[1024,512]{1,0:T(8,128)(2,1)S(1)}, bf16[1024,512]{1,0:T(8,128)(2,1)}, u32[]{:S(2)}) copy-start(bf16[1024,512]{1,0:T(8,128)(2,1)} %param.12) | copy-start | bytes 3145732
  0.7 12.1 %copy-start.12 = (s32[1,1,8,64]{3,2,1,0:T(8,128)S(1)}, s32[1,1,8,64]{3,2,1,0:T(8,128)}, u32[]{:S(2)}) copy-start(s32[1,1,8,64]{3,2,1,0:T(8,128)} %param.21) | copy-start | bytes 6148
  0.7 12.1 %copy-start.14 = (s32[1,1,8]{2,1,0:T(1,128)S(1)}, s32[1,1,8]{2,1,0:T(1,128)}, u32[]{:S(2)}) copy-start(s32[1,1,8]{2,1,0:T(1,128)} %param.22) | copy-start | bytes 100
  0.7 53.5 %collective-permute-start = (bf16[1024,512]{1,0:T(8,128)(2,1)}, bf16[1024,512]{1,0:T(8,128)(2,1)}, u32[]{:S(2)}, u32[]{:S(2)}) collective-permute-start(bf16[1024,512]{1,0:T(8,128)(2,1)} %param.12), channel_id=1, source_target_pairs={{2,0},{1,3},{0,1},{3,2},{6,4},{5,7},{4,5},{7,6},{10,8},{9,11},{8,9... | collective-permute-start | bytes 3145736 | tf_op jit(solution)/shard_map/ppermute | solution.py:160
  6.0 33.6 %collective-permute-start.1 = (bf16[512,512]{1,0:T(8,128)(2,1)}, bf16[512,512]{1,0:T(8,128)(2,1)}, u32[]{:S(2)}, u32[]{:S(2)}) collective-permute-start(bf16[512,512]{1,0:T(8,128)(2,1)} %get-tuple-element.21), channel_id=1, source_target_pairs={{1,0},{2,3},{3,1},{0,2},{5,4},{6,7},{7,5},{4,6},{9,8},{10,11},{11,... | collective-permute-start | bytes 1572872 | tf_op jit(solution)/shard_map/ppermute | solution.py:160
  7.1 52.6 %collective-permute-start.4 = (bf16[512,512]{1,0:T(8,128)(2,1)}, bf16[512,512]{1,0:T(8,128)(2,1)}, u32[]{:S(2)}, u32[]{:S(2)}) collective-permute-start(bf16[512,512]{1,0:T(8,128)(2,1)} %get-tuple-element.21), channel_id=1, source_target_pairs={{1,2},{2,1},{5,6},{6,5},{9,10},{10,9},{13,14},{14,13},{17,18},{18,... | collective-permute-start | bytes 1572872 | tf_op jit(solution)/shard_map/ppermute | solution.py:160
  8.6 42.3 %collective-permute-start.2 = (bf16[512,512]{1,0:T(8,128)(2,1)}, bf16[512,512]{1,0:T(8,128)(2,1)}, u32[]{:S(2)}, u32[]{:S(2)}) collective-permute-start(bf16[512,512]{1,0:T(8,128)(2,1)} %get-tuple-element.20), channel_id=1, source_target_pairs={{1,0},{2,3},{3,1},{0,2},{5,4},{6,7},{7,5},{4,6},{9,8},{10,11},{11,... | collective-permute-start | bytes 1572872 | tf_op jit(solution)/shard_map/ppermute | solution.py:160
  12.0 52.1 %collective-permute-start.6 = (bf16[512,512]{1,0:T(8,128)(2,1)}, bf16[512,512]{1,0:T(8,128)(2,1)S(1)}, u32[]{:S(2)}, u32[]{:S(2)}) collective-permute-start(bf16[512,512]{1,0:T(8,128)(2,1)} %get-tuple-element.20), channel_id=1, source_target_pairs={{1,2},{2,1},{5,6},{6,5},{9,10},{10,9},{13,14},{14,13},{17,18},{18,... | collective-permute-start | bytes 1572872 | tf_op jit(solution)/shard_map/ppermute | solution.py:160
  13.0 5.7 %copy-start.13 = (s32[128]{0:T(128)S(1)}, s32[128]{0:T(128)}, u32[]{:S(2)}) copy-start(s32[128]{0:T(128)} %param.17) | copy-start | bytes 1540
  14.5 22.4 %all-to-all-start = ((bf16[8,64,512]{2,1,0:T(8,128)(2,1)}), bf16[8,64,512]{2,1,0:T(8,128)(2,1)}, u32[]{:S(2)}, u32[]{:S(2)}) async-start(bf16[8,64,512]{2,1,0:T(8,128)(2,1)} %bitcast.1), calls=%async_computation | async-start | bytes 1048576 | tf_op jit(solution)/shard_map/all_to_all | solution.py:197
  31.9 4.3 %copy-start.8 = (bf16[1024,512]{1,0:T(8,128)(2,1)S(1)}, bf16[1024,512]{1,0:T(8,128)(2,1)}, u32[]{:S(2)}) copy-start(bf16[1024,512]{1,0:T(8,128)(2,1)} %param.12) | copy-start | bytes 3145732
  39.6 22.4 %collective-permute-start.3 = (bf16[512,512]{1,0:T(8,128)(2,1)}, bf16[512,512]{1,0:T(8,128)(2,1)S(1)}, u32[]{:S(2)}, u32[]{:S(2)}) collective-permute-start(bf16[512,512]{1,0:T(8,128)(2,1)} %collective-permute-done.1), channel_id=1, source_target_pairs={{1,0},{2,3},{5,4},{6,7},{9,8},{10,11},{13,12},{14,15},{17,16},{18,... | collective-permute-start | bytes 1572872 | tf_op jit(solution)/shard_map/ppermute | solution.py:160
  50.8 22.3 %collective-permute-start.5 = (bf16[512,512]{1,0:T(8,128)(2,1)}, bf16[512,512]{1,0:T(8,128)(2,1)S(1)}, u32[]{:S(2)}, u32[]{:S(2)}) collective-permute-start(bf16[512,512]{1,0:T(8,128)(2,1)} %collective-permute-done.2), channel_id=1, source_target_pairs={{1,0},{2,3},{5,4},{6,7},{9,8},{10,11},{13,12},{14,15},{17,16},{18,... | collective-permute-start | bytes 1572872 | tf_op jit(solution)/shard_map/ppermute | solution.py:160
  54.2 3.3 %copy-start.10 = (f32[1024,512]{1,0:T(8,128)S(1)}, f32[1024,512]{1,0:T(8,128)}, u32[]{:S(2)}) copy-start(f32[1024,512]{1,0:T(8,128)} %fusion.13) | copy-start | bytes 6291460
  59.7 13.4 %copy-start.3 = (bf16[1024,512]{1,0:T(8,128)(2,1)S(1)}, bf16[1024,512]{1,0:T(8,128)(2,1)}, u32[]{:S(2)}) copy-start(bf16[1024,512]{1,0:T(8,128)(2,1)} %cot_ref.1) | copy-start | bytes 3145732
  59.7 13.4 %copy-start.4 = (bf16[512,512]{1,0:T(8,128)(2,1)S(1)}, bf16[512,512]{1,0:T(8,128)(2,1)}, u32[]{:S(2)}) copy-start(bf16[512,512]{1,0:T(8,128)(2,1)} %w_ref.1) | copy-start | bytes 1572868
  64.1 17.2 %copy-start.11 = (bf16[1024,512]{1,0:T(8,128)(2,1)S(1)}, bf16[1024,512]{1,0:T(8,128)(2,1)}, u32[]{:S(2)}) copy-start(bf16[1024,512]{1,0:T(8,128)(2,1)} %get-tuple-element.12) | copy-start | bytes 3145732
  81.2 1.0 copy-start.5
  81.3 9.6 %copy-start.1 = (bf16[1024,512]{1,0:T(8,128)(2,1)}, bf16[1024,512]{1,0:T(8,128)(2,1)S(1)}, u32[]{:S(2)}) copy-start(bf16[1024,512]{1,0:T(8,128)(2,1)S(1)} %get-tuple-element.14) | copy-start | bytes 3145732
  82.2 7.8 %copy-start.9 = (bf16[1024,512]{1,0:T(8,128)(2,1)S(1)}, bf16[1024,512]{1,0:T(8,128)(2,1)}, u32[]{:S(2)}) copy-start(bf16[1024,512]{1,0:T(8,128)(2,1)} %param.12) | copy-start | bytes 3145732
  86.2 26.7 %collective-permute-start.9 = (bf16[1024,512]{1,0:T(8,128)(2,1)}, bf16[1024,512]{1,0:T(8,128)(2,1)}, u32[]{:S(2)}, u32[]{:S(2)}) collective-permute-start(bf16[1024,512]{1,0:T(8,128)(2,1)} %get-tuple-element.17), channel_id=1, source_target_pairs={{0,1},{3,2},{4,5},{7,6},{8,9},{11,10},{12,13},{15,14},{16,17},{19,... | collective-permute-start | bytes 3145736 | tf_op jit(solution)/shard_map/ppermute | solution.py:160
  93.3 3.9 %copy-start.6 = (bf16[1024,512]{1,0:T(8,128)(2,1)S(1)}, bf16[1024,512]{1,0:T(8,128)(2,1)}, u32[]{:S(2)}) copy-start(bf16[1024,512]{1,0:T(8,128)(2,1)} %copy-done.5) | copy-start | bytes 3145732
  93.3 26.1 %all-to-all-start.1 = ((bf16[8,192,512]{2,1,0:T(8,128)(2,1)}), bf16[8,192,512]{2,1,0:T(8,128)(2,1)S(1)}, u32[]{:S(2)}, u32[]{:S(2)}) async-start(bf16[8,192,512]{2,1,0:T(8,128)(2,1)} %pad_maximum_fusion), calls=%async_computation.1 | async-start | bytes 3145728 | tf_op jit(solution)/shard_map/all_to_all | solution.py:224
  97.2 5.3 %copy-start.2 = (bf16[1024,512]{1,0:T(8,128)(2,1)S(1)}, bf16[1024,512]{1,0:T(8,128)(2,1)}, u32[]{:S(2)}) copy-start(bf16[1024,512]{1,0:T(8,128)(2,1)} %copy-done.1) | copy-start | bytes 3145732
  100.2 35.3 %collective-permute-start.7 = (bf16[1024,512]{1,0:T(8,128)(2,1)}, bf16[1024,512]{1,0:T(8,128)(2,1)}, u32[]{:S(2)}, u32[]{:S(2)}) collective-permute-start(bf16[1024,512]{1,0:T(8,128)(2,1)} %get-tuple-element.17), channel_id=1, source_target_pairs={{1,2},{2,1},{5,6},{6,5},{9,10},{10,9},{13,14},{14,13},{17,18},{18,... | collective-permute-start | bytes 3145736 | tf_op jit(solution)/shard_map/ppermute | solution.py:160
  101.8 33.6 %collective-permute-start.8 = (bf16[1024,512]{1,0:T(8,128)(2,1)}, bf16[1024,512]{1,0:T(8,128)(2,1)}, u32[]{:S(2)}, u32[]{:S(2)}) collective-permute-start(bf16[1024,512]{1,0:T(8,128)(2,1)} %fusion.15), channel_id=1, source_target_pairs={{0,2},{3,1},{1,0},{2,3},{4,6},{7,5},{5,4},{6,7},{8,10},{11,9},{9,8... | collective-permute-start | bytes 3145736 | tf_op jit(solution)/shard_map/ppermute | solution.py:160
  115.6 66.2 %collective-permute-start.10 = (bf16[512,512]{1,0:T(8,128)(2,1)}, bf16[512,512]{1,0:T(8,128)(2,1)}, u32[]{:S(2)}, u32[]{:S(2)}) collective-permute-start(bf16[512,512]{1,0:T(8,128)(2,1)} %get-tuple-element.19), channel_id=1, source_target_pairs={{0,1},{3,2},{1,3},{2,0},{4,5},{7,6},{5,7},{6,4},{8,9},{11,10},{9,1... | collective-permute-start | bytes 1572872 | tf_op jit(solution)/shard_map/ppermute | solution.py:160
  118.0 65.9 %collective-permute-start.11 = (bf16[512,512]{1,0:T(8,128)(2,1)}, bf16[512,512]{1,0:T(8,128)(2,1)}, u32[]{:S(2)}, u32[]{:S(2)}) collective-permute-start(bf16[512,512]{1,0:T(8,128)(2,1)} %get-tuple-element.18), channel_id=1, source_target_pairs={{0,1},{3,2},{1,3},{2,0},{4,5},{7,6},{5,7},{6,4},{8,9},{11,10},{9,1... | collective-permute-start | bytes 1572872 | tf_op jit(solution)/shard_map/ppermute | solution.py:160
  122.5 54.5 %all-to-all-start.2 = ((f32[4,2,16,512]{3,2,1,0:T(8,128)}), f32[4,2,16,512]{3,2,1,0:T(8,128)S(1)}, u32[]{:S(2)}, u32[]{:S(2)}) async-start(f32[4,2,16,512]{3,2,1,0:T(8,128)} %bitcast.10), calls=%async_computation.2 | async-start | bytes 524288 | tf_op jit(solution)/shard_map/all_to_all | solution.py:228
  177.9 13.5 %all-to-all-start.3 = ((f32[8,2,16,512]{3,2,1,0:T(8,128)}), f32[8,2,16,512]{3,2,1,0:T(8,128)S(1)}, u32[]{:S(2)}, u32[]{:S(2)}) async-start(f32[8,2,16,512]{3,2,1,0:T(8,128)} %broadcast_in_dim.2), calls=%async_computation.3 | async-start | bytes 1048576 | tf_op jit(solution)/shard_map/all_to_all | solution.py:231

commit v2 on v1

--- a/solution.py
+++ b/solution.py
@@ -8,12 +8,13 @@
 from jax.sharding import PartitionSpec as P
 
 
-ROW_STEP = 256
+ROW_STEP = 512
 
 
 def densify_kernel(
-    local_rows, local_cols, halo_rows, halo_cols, local_ref, halo_ref, dense_ref, hdense_ref, acc, hacc
+    local_rows, local_cols, halo_rows, halo_cols, local_ref, halo_ref, *refs
 ):
+    *dense_refs, hdense_ref, acc, hacc = refs
     tile_size = local_ref.shape[1]
 
     def place(rows, cols, tiles, total):
@@ -28,22 +29,22 @@
         lax.fori_loop(0, tiles.shape[0], step, 0)
 
     place(local_rows, local_cols, local_ref, acc)
-    dense_ref[...] = acc[...].astype(dense_ref.dtype)
+    for i, ref in enumerate(dense_refs):
+        ref[...] = acc[:, i * ref.shape[1] : (i + 1) * ref.shape[1]].astype(ref.dtype)
     place(halo_rows, halo_cols, halo_ref, hacc)
     hdense_ref[...] = hacc[...].astype(hdense_ref.dtype)
 
 
-def densify(local_tiles, local_rows, local_cols, halo_tiles, halo_rows, halo_cols, rows, cols, hcols):
+def densify(local_tiles, local_rows, local_cols, halo_tiles, halo_rows, halo_cols, rows, slots, hcols):
     smem = pl.BlockSpec(memory_space=pltpu.SMEM)
     vmem = pl.BlockSpec(memory_space=pltpu.VMEM)
-    return pl.pallas_call(
+    cols = rows * slots
+    *parts, halo = pl.pallas_call(
         densify_kernel,
-        out_shape=(
-            jax.ShapeDtypeStruct((rows, cols), jnp.bfloat16),
-            jax.ShapeDtypeStruct((rows, hcols), jnp.bfloat16),
-        ),
+        out_shape=(jax.ShapeDtypeStruct((rows, rows), jnp.bfloat16),) * slots
+        + (jax.ShapeDtypeStruct((rows, hcols), jnp.bfloat16),),
         in_specs=[smem] * 4 + [vmem] * 2,
-        out_specs=(vmem, vmem),
+        out_specs=(vmem,) * (slots + 1),
         scratch_shapes=[pltpu.VMEM((rows, cols), jnp.float32), pltpu.VMEM((rows, hcols), jnp.float32)],
         compiler_params=pltpu.CompilerParams(vmem_limit_bytes=60 << 20),
         cost_estimate=pl.CostEstimate(
@@ -51,6 +52,7 @@
         ),
         name="densify",
     )(local_rows, local_cols, halo_rows, halo_cols, local_tiles, halo_tiles)
+    return parts, halo
 
 
 def dot(a, b):
@@ -63,63 +65,39 @@
 
 def middle_kernel(
     acc_ref, dense_ref, outer_ref, inner_ref, pre_ref, cot_ref, w_ref,
-    out_ref, neighbour_ref, grad_ref, agg_ref, term_ref, total, far,
+    out_ref, neighbour_ref, grad_ref, agg_ref, term_ref,
 ):
-    step = pl.program_id(0)
-    half = far.shape[0]
-
-    @pl.when(step == 0)
-    def _():
-        far[...] = outer_ref[...] + inner_ref[...]
-
-    dense = dense_ref[...]
-    neighbour = (acc_ref[...] + dot(dense[:, -half:], far[...])).astype(jnp.bfloat16)
-    neighbour_ref[...] = neighbour
-    preact = pre_ref[...] + dot(neighbour, w_ref[...])
-    sigmoid_pre = jax.nn.sigmoid(preact)
-    out_ref[...] = (preact * sigmoid_pre).astype(out_ref.dtype)
-    slope = sigmoid_pre * (1.0 + preact * (1.0 - sigmoid_pre))
-    grad = (cot_ref[...].astype(jnp.float32) * slope).astype(jnp.bfloat16)
-    grad_ref[...] = grad
-    agg = lax.dot_general(
-        grad, w_ref[...], (((1,), (1,)), ((), ())), preferred_element_type=jnp.float32
-    ).astype(jnp.bfloat16)
-    agg_ref[...] = agg
-    term = dot_t(dense, agg)
-
-    @pl.when(step == 0)
-    def _():
-        total[...] = term
-
-    @pl.when(step > 0)
-    def _():
-        total[...] += term
-
-    @pl.when(step == pl.num_programs(0) - 1)
-    def _():
-        term_ref[...] = total[...].astype(term_ref.dtype)
-
-
-def middle(acc, dense, slot, outer, inner, pre_self, cotangent, w_neigh):
+    rows, half = acc_ref.shape[0], outer_ref.shape[0]
+    step = math.gcd(rows, ROW_STEP)
+    far = outer_ref[...] + inner_ref[...]
+    w = w_ref[...]
+    for start in range(0, rows, step):
+        at = slice(start, start + step)
+        neighbour = acc_ref[at, :] + dot(dense_ref[at, rows - half :], far)
+        neighbour = neighbour.astype(jnp.bfloat16)
+        neighbour_ref[at, :] = neighbour
+        preact = pre_ref[at, :] + dot(neighbour, w)
+        sigmoid_pre = jax.nn.sigmoid(preact)
+        out_ref[at, :] = (preact * sigmoid_pre).astype(out_ref.dtype)
+        slope = sigmoid_pre * (1.0 + preact * (1.0 - sigmoid_pre))
+        grad = (cot_ref[at, :].astype(jnp.float32) * slope).astype(jnp.bfloat16)
+        grad_ref[at, :] = grad
+        agg_ref[at, :] = lax.dot_general(
+            grad, w, (((1,), (1,)), ((), ())), preferred_element_type=jnp.float32
+        ).astype(jnp.bfloat16)
+    for start in range(0, rows, step):
+        at = slice(start, start + step)
+        term_ref[at, :] = dot_t(dense_ref[:, at], agg_ref[...]).astype(term_ref.dtype)
+
+
+def middle(acc, dense, outer, inner, pre_self, cotangent, w_neigh):
     rows, width = acc.shape
-    step = math.gcd(rows, ROW_STEP)
-    by_rows = pl.BlockSpec((step, width), lambda i: (i, 0))
-    like = jax.ShapeDtypeStruct((rows, width), jnp.bfloat16)
+    vmem = pl.BlockSpec(memory_space=pltpu.VMEM)
     return pl.pallas_call(
         middle_kernel,
-        grid=(rows // step,),
-        out_shape=(like,) * 5,
-        in_specs=[
-            by_rows,
-            pl.BlockSpec((step, rows), lambda i: (i, slot)),
-            pl.BlockSpec(outer.shape, lambda i: (0, 0)),
-            pl.BlockSpec(outer.shape, lambda i: (0, 0)),
-            by_rows,
-            by_rows,
-            pl.BlockSpec(w_neigh.shape, lambda i: (0, 0)),
-        ],
-        out_specs=(by_rows,) * 4 + (pl.BlockSpec((rows, width), lambda i: (0, 0)),),
-        scratch_shapes=[pltpu.VMEM((rows, width), jnp.float32), pltpu.VMEM(outer.shape, jnp.bfloat16)],
+        out_shape=(jax.ShapeDtypeStruct((rows, width), jnp.bfloat16),) * 5,
+        in_specs=[vmem] * 7,
+        out_specs=(vmem,) * 5,
         compiler_params=pltpu.CompilerParams(vmem_limit_bytes=40 << 20),
         cost_estimate=pl.CostEstimate(
             flops=4 * rows * width * (rows + width), bytes_accessed=18 << 20, transcendentals=rows * width
@@ -172,7 +150,7 @@
     slot_cols = slot * blocks + local_cols % blocks
     cut_list = cut_rows[0, 0]
     halo_size = cut_list.shape[0] * cut_list.shape[1]
-    dense, hdense = densify(
+    parts, hdense = densify(
         local_tiles,
         local_rows,
         slot_cols,
@@ -180,12 +158,12 @@
         halo_rows,
         halo_cols,
         row_count,
-        n * row_count,
+        n,
         halo_size,
     )
 
     def part(slot_id):
-        return dense[:, slot_id * row_count : (slot_id + 1) * row_count]
+        return parts[slot_id]
 
     slot_index = jnp.arange(cut_list.shape[1], dtype=jnp.int32)
     live = slot_index[None, :] < cut_counts[0, 0][:, None]
@@ -207,7 +185,7 @@
     summed = lax.optimization_barrier(summed)
     summed = summed + dot(part(3)[:, :half], third_a + inner_a)
     out, neighbour, grad_pre, grad_agg, term = middle(
-        summed, dense, 3, third_b, inner_b, pre_self, cotangent, w_neigh
+        summed, part(3), third_b, inner_b, pre_self, cotangent, w_neigh
     )
 
     passed = move(term, inward)
@@ -225,8 +203,9 @@
     slots = cut_list.shape[1]
     returned = both[:, :slots].reshape(halo_size, width)
     both = jnp.sum(both[:, slots:].astype(jnp.float32), axis=0).reshape(n, 2, share, width)
+    both = both.astype(jnp.bfloat16)
     both = lax.all_to_all(both, "rep", split_axis=0, concat_axis=0, tiled=True)
-    both = jnp.sum(both, axis=0)
+    both = jnp.sum(both.astype(jnp.float32), axis=0)
     both = jnp.broadcast_to(both[None], (dom, 2, share, width))
     both = lax.all_to_all(
         both,
@@ -242,18 +221,19 @@
     second_back = move(second_term, second_out)
     first_term = lax.optimization_barrier(dot_t(part(1), grad_agg))
     first_term = first_term + passed.astype(jnp.float32)
-    last_a = move(first_term[:half].astype(jnp.bfloat16), first_out)
-    last_b = move(first_term[half:].astype(jnp.bfloat16), first_out)
+    most = row_count - row_count // 4
+    last_a = move(first_term[:most].astype(jnp.bfloat16), first_out)
+    last_b = move(first_term[most:].astype(jnp.bfloat16), first_out)
 
     d_x = dot(grad_pre, w_self.T) + dot_t(part(0), grad_agg)
     d_x = d_x + dot_t(selector, returned)
     d_x = d_x + near.astype(jnp.float32)
     d_x = d_x + second_back.astype(jnp.float32)
     d_x = lax.optimization_barrier(d_x)
-    base = jnp.concatenate([last_a.astype(jnp.float32), jnp.zeros((row_count - half, width))])
+    base = jnp.concatenate([last_a.astype(jnp.float32), jnp.zeros((row_count - most, width))])
     base = lax.optimization_barrier((d_x + base).astype(jnp.bfloat16))
-    last = (d_x[half:] + last_b.astype(jnp.float32)).astype(jnp.bfloat16)
-    d_x = lax.dynamic_update_slice_in_dim(base, last, half, 0)
+    last = (d_x[most:] + last_b.astype(jnp.float32)).astype(jnp.bfloat16)
+    d_x = lax.dynamic_update_slice_in_dim(base, last, most, 0)
     return (out, d_x, d_w_self, d_w_neigh)
 
 

time: 193 us -> 173 us (0.90)
  waiting for transfers between devices: 77.7 us -> 66.5 us
  matrix products: 36 us -> 31.7 us
  Pallas kernels: 20.8 us -> 16.9 us
    all_to_all x1, waiting for transfers between devices: 37.2 us -> 23.8 us  [per_device(): both = lax.all_to_all(both, 'rep', split_axis=0, concat_axis=0, tiled=True)]
    pallas_call x2, Pallas kernels: 20.8 us -> 16.9 us  [the longest x1 12.6 us: densify(): pl.pallas_call(densify_kernel, out_shape=(jax.ShapeDtypeStruct((rows, row...]
    dot_general x7, matrix products: 15.6 us -> 12.5 us  [dot_t(): lax.dot_general(a, b, (((0,), (0,)), ((), ())), preferred_element_type=jn...]
  transfers between devices with their start and end apart: 16 -> 16, of which waited for: 8 -> 9; matrix products, arithmetic and copies ran while one was open for 26% -> 26% of each run, Pallas kernels for 7% -> 7%
where the time goes in v2:
time: 173 us; the launch traced here: 172 us
  waiting for transfers between devices  66.5 us (38%)
  starting transfers between devices  39.1 us (23%)
  matrix products  31.7 us (18%)
  Pallas kernels  16.9 us (10%)
  other arithmetic  11.7 us (7%)
  local copies, waits for them, and re-layouts  5.51 us (3%)
    ppermute x12, waiting for transfers between devices, move(): return lax.ppermute(value, 'rep', pairs)  36.8 us
    all_to_all x1, waiting for transfers between devices, per_device(): both = lax.all_to_all(both, 'rep', split_axis=0, concat_axis=0, tiled=True)  23.8 us
    ppermute x12, starting transfers between devices, move(): return lax.ppermute(value, 'rep', pairs)  22.8 us
    dot_general x9, matrix products, dot(): return jnp.dot(a, b, preferred_element_type=jnp.float32)  19.2 us
    pallas_call x1, Pallas kernels, densify(): pl.pallas_call(densify_kernel, out_shape=(jax.ShapeDtypeStruct((rows, row...  12.6 us
    dot_general x7, matrix products, dot_t(): lax.dot_general(a, b, (((0,), (0,)), ((), ())), preferred_element_type=jn...  12.5 us
    all_to_all x2, starting transfers between devices, per_device(): both = lax.all_to_all(both, 'dom', split_axis=0, concat_axis=0, tiled=True)  7.58 us
    all_to_all x2, waiting for transfers between devices, per_device(): both = lax.all_to_all(both, 'dom', split_axis=0, concat_axis=0, tiled=True)  5.8 us
  transfers between devices with their start and end apart: 16, of which 9 were waited for; matrix products, arithmetic and copies ran while one was open for 26% of the time, Pallas kernels for 7%

profile of v2, /device:TPU:0, one launch (start us, length us, event | category | flops | bytes accessed | tf_op | source)
XLA Modules:
  0.0 172.4 jit_solution(12735944807240534583)
XLA Ops:
  0.7 3.1 %collective-permute-start = (bf16[1024,512]{1,0:T(8,128)(2,1)}, bf16[1024,512]{1,0:T(8,128)(2,1)}, u32[]{:S(2)}, u32[]{:S(2)}) collective-permute-start(bf16[1024,512]{1,0:T(8,128)(2,1)} %param.12), channel_id=1, source_target_pairs={{2,0},{1,3},{0,1},{3,2},{6,4},{5,7},{4,5},{7,6},{10,8},{9,11},{8,9... | collective-permute-start | bytes 3145736 | tf_op jit(solution)/shard_map/ppermute | solution.py:138
  3.8 2.3 %fusion.25 = (bf16[512,512]{1,0:T(8,128)(2,1)}, bf16[512,512]{1,0:T(8,128)(2,1)}) fusion(bf16[1024,512]{1,0:T(8,128)(2,1)} %param.12), kind=kLoop, calls=%fused_computation.41 | loop fusion | bytes 2097152 | tf_op jit(solution)/shard_map/slice | solution.py:141
  8.7 3.4 %collective-permute-start.2 = (bf16[512,512]{1,0:T(8,128)(2,1)}, bf16[512,512]{1,0:T(8,128)(2,1)}, u32[]{:S(2)}, u32[]{:S(2)}) collective-permute-start(bf16[512,512]{1,0:T(8,128)(2,1)} %get-tuple-element.24), channel_id=1, source_target_pairs={{1,0},{2,3},{3,1},{0,2},{5,4},{6,7},{7,5},{4,6},{9,8},{10,11},{11,... | collective-permute-start | bytes 1572872 | tf_op jit(solution)/shard_map/ppermute | solution.py:138
  14.6 4.1 %all-to-all-start = ((bf16[8,64,512]{2,1,0:T(8,128)(2,1)}), bf16[8,64,512]{2,1,0:T(8,128)(2,1)}, u32[]{:S(2)}, u32[]{:S(2)}) async-start(bf16[8,64,512]{2,1,0:T(8,128)(2,1)} %bitcast.1), calls=%async_computation | async-start | bytes 1048576 | tf_op jit(solution)/shard_map/all_to_all | solution.py:175
  19.3 12.6 %densify.1 = (bf16[1024,1024]{1,0:T(8,128)(2,1)}, bf16[1024,1024]{1,0:T(8,128)(2,1)}, bf16[1024,1024]{1,0:T(8,128)(2,1)}, bf16[1024,1024]{1,0:T(8,128)(2,1)}, bf16[1024,512]{1,0:T(8,128)(2,1)}) custom-call(s32[128]{0:T(128)} %local_rows.1, s32[128]{0:T(128)} %fusion.24.local_cols, s32[96]{0:T(128)} %halo_rows.1, s32[96]{0:T(128)} %halo_cols.1, ...), custom_call_target="tpu_custom_call" | custom-call | flops 8388608 | bytes 18874368 | tf_op jit(solution)/shard_map/densify/pallas_call | solution.py:42
  31.8 4.3 %fusion.27 = f32[1024,512]{1,0:T(8,128)} fusion(bf16[1024,1024]{1,0:T(8,128)(2,1)} %get-tuple-element.14, bf16[1024,512]{1,0:T(8,128)(2,1)S(1)} %copy-done.9), kind=kOutput, calls=%fused_computation.43 | convolution fusion | flops 1073741824 | bytes 5242880 | tf_op jit(solution)/shard_map/dot_general | solution.py:59
  36.9 2.2 %fusion.28 = f32[1024,512]{1,0:T(8,128)S(1)} fusion(bf16[1024,512]{1,0:T(8,128)(2,1)} %get-tuple-element.15, bf16[512,512]{1,0:T(8,128)(2,1)} %bitcast.2), kind=kOutput, calls=%fused_computation.44 | convolution fusion | flops 536870912 | bytes 3670016 | tf_op jit(solution)/shard_map/dot_general | solution.py:59
  41.0 9.8 %collective-permute-done.2 = bf16[512,512]{1,0:T(8,128)(2,1)} collective-permute-done((bf16[512,512]{1,0:T(8,128)(2,1)}, bf16[512,512]{1,0:T(8,128)(2,1)}, u32[]{:S(2)}, u32[]{:S(2)}) %collective-permute-start.2) | collective-permute-done | bytes 524320 | tf_op jit(solution)/shard_map/ppermute | solution.py:138
  52.3 1.7 %fusion.15 = f32[1024,512]{1,0:T(8,128)S(1)} fusion(bf16[512,512]{1,0:T(8,128)(2,1)} %collective-permute-done.1, bf16[1024,1024]{1,0:T(8,128)(2,1)S(1)} %copy-done.12), kind=kOutput, calls=%fused_computation.22 | convolution fusion | flops 536870912 | bytes 3670016 | tf_op jit(solution)/shard_map/dot_general | solution.py:59
  54.1 2.6 %fusion.29 = f32[1024,512]{1,0:T(8,128)S(1)} fusion(bf16[1024,1024]{1,0:T(8,128)(2,1)S(1)} %copy-done.19, bf16[1024,512]{1,0:T(8,128)(2,1)} %collective-permute-done), kind=kOutput, calls=%fused_computation.45 | convolution fusion | flops 1073741824 | bytes 5242880 | tf_op jit(solution)/shard_map/dot_general | solution.py:59
  56.7 2.1 %add_add_fusion = f32[1024,512]{1,0:T(8,128)S(1)} fusion(f32[1024,512]{1,0:T(8,128)S(1)} %fusion.15, f32[1024,512]{1,0:T(8,128)S(1)} %fusion.29, f32[1024,512]{1,0:T(8,128)S(1)} %copy-done.14, f32[1024,512]{1,0:T(8,128)S(1)} %fusion.28, bf16[512,512]{1,0:T(8,128)(2,1)} %collective-permute-done.2, bf16[1024,1024]{1,0:T(8,128)(2,1)S(1)} %copy-done.12), kind=kOutput, calls=%fused_computation.3 | convolution fusion | flops 538968064 | bytes 12058624 | tf_op jit(solution)/shard_map/dot_general | solution.py:59
  58.9 3.1 %collective-permute-done.3 = bf16[512,512]{1,0:T(8,128)(2,1)S(1)} collective-permute-done((bf16[512,512]{1,0:T(8,128)(2,1)}, bf16[512,512]{1,0:T(8,128)(2,1)S(1)}, u32[]{:S(2)}, u32[]{:S(2)}) %collective-permute-start.3) | collective-permute-done | bytes 524320 | tf_op jit(solution)/shard_map/ppermute | solution.py:138
  62.0 1.9 %convolution_add_fusion.acc_ref = f32[1024,512]{1,0:T(8,128)S(1)} fusion(f32[1024,512]{1,0:T(8,128)S(1)} %add_add_fusion, bf16[1024,1024]{1,0:T(8,128)(2,1)S(1)} %copy-done.3, bf16[512,512]{1,0:T(8,128)(2,1)S(1)} %collective-permute-done.3, bf16[512,512]{1,0:T(8,128)(2,1)} %collective-permute-done.4), kind=kOutput, calls=%fused_computation.8 | convolution fusion | flops 537657344 | bytes 6291456 | tf_op jit(solution)/shard_map/dot_general | solution.py:59
  63.9 9.2 %collective-permute-done.5.outer_ref = bf16[512,512]{1,0:T(8,128)(2,1)S(1)} collective-permute-done((bf16[512,512]{1,0:T(8,128)(2,1)}, bf16[512,512]{1,0:T(8,128)(2,1)S(1)}, u32[]{:S(2)}, u32[]{:S(2)}) %collective-permute-start.5) | collective-permute-done | bytes 524320 | tf_op jit(solution)/shard_map/ppermute | solution.py:138
  73.1 4.4 %middle.1 = (bf16[1024,512]{1,0:T(8,128)(2,1)}, bf16[1024,512]{1,0:T(8,128)(2,1)S(1)}, bf16[1024,512]{1,0:T(8,128)(2,1)S(1)}, bf16[1024,512]{1,0:T(8,128)(2,1)S(1)}, bf16[1024,512]{1,0:T(8,128)(2,1)}) custom-call(f32[1024,512]{1,0:T(8,128)S(1)} %convolution_add_fusion.acc_ref, bf16[1024,1024]{1,0:T(8,128)(2,1)S(1)} %copy-done.3, ...), custom_call_target="tpu_custom_call" | custom-call | flops 3221225472 | bytes 18874368 | tf_op jit(solution)/shard_map/middle/pallas_call | solution.py:96
  77.5 2.7 %fusion.33 = f32[1024,512]{1,0:T(8,128)} fusion(bf16[1024,1024]{1,0:T(8,128)(2,1)S(1)} %copy-done.12, bf16[1024,512]{1,0:T(8,128)(2,1)S(1)} %get-tuple-element.21), kind=kOutput, calls=%fused_computation.49 | convolution fusion | flops 1073741824 | bytes 5242880 | tf_op jit(solution)/shard_map/dot_general | solution.py:63
  80.9 3.9 %collective-permute-start.9 = (bf16[1024,512]{1,0:T(8,128)(2,1)}, bf16[1024,512]{1,0:T(8,128)(2,1)}, u32[]{:S(2)}, u32[]{:S(2)}) collective-permute-start(bf16[1024,512]{1,0:T(8,128)(2,1)} %get-tuple-element.23), channel_id=1, source_target_pairs={{0,1},{3,2},{4,5},{7,6},{8,9},{11,10},{12,13},{15,14},{16,17},{19,... | collective-permute-start | bytes 3145736 | tf_op jit(solution)/shard_map/ppermute | solution.py:138
  84.8 1.6 collective-permute-start.7
  89.7 3.9 %all-to-all-start.1 = ((bf16[8,192,512]{2,1,0:T(8,128)(2,1)}), bf16[8,192,512]{2,1,0:T(8,128)(2,1)S(1)}, u32[]{:S(2)}, u32[]{:S(2)}) async-start(bf16[8,192,512]{2,1,0:T(8,128)(2,1)} %pad_maximum_fusion), calls=%async_computation.1 | async-start | bytes 3145728 | tf_op jit(solution)/shard_map/all_to_all | solution.py:202
  93.6 4.0 %convolution_convert_fusion = bf16[1024,512]{1,0:T(8,128)(2,1)} fusion(bf16[1024,1024]{1,0:T(8,128)(2,1)} %get-tuple-element.16, bf16[1024,512]{1,0:T(8,128)(2,1)S(1)} %copy-done.7), kind=kOutput, calls=%fused_computation.10 | convolution fusion | flops 1074266112 | bytes 4194304 | tf_op jit(solution)/shard_map/dot_general | solution.py:63
  98.1 2.7 %fusion.32 = f32[1024,512]{1,0:T(8,128)} fusion(bf16[1024,1024]{1,0:T(8,128)(2,1)S(1)} %copy-done.18, bf16[1024,512]{1,0:T(8,128)(2,1)S(1)} %copy-done.7), kind=kOutput, calls=%fused_computation.48 | convolution fusion | flops 1073741824 | bytes 5242880 | tf_op jit(solution)/shard_map/dot_general | solution.py:63
  100.8 2.1 %fusion.31 = f32[1024,512]{1,0:T(8,128)} fusion(bf16[1024,512]{1,0:T(8,128)(2,1)S(1)} %copy-done.2, bf16[512,512]{1,0:T(8,128)(2,1)S(1)} %copy-done), kind=kOutput, calls=%fused_computation.47 | convolution fusion | flops 536870912 | bytes 3670016 | tf_op jit(solution)/shard_map/dot_general | solution.py:59
  102.8 4.8 %collective-permute-done.9 = bf16[1024,512]{1,0:T(8,128)(2,1)} collective-permute-done((bf16[1024,512]{1,0:T(8,128)(2,1)}, bf16[1024,512]{1,0:T(8,128)(2,1)}, u32[]{:S(2)}, u32[]{:S(2)}) %collective-permute-start.9) | collective-permute-done | bytes 1048608 | tf_op jit(solution)/shard_map/ppermute | solution.py:138
  110.2 2.8 %collective-permute-start.10 = (bf16[768,512]{1,0:T(8,128)(2,1)}, bf16[768,512]{1,0:T(8,128)(2,1)}, u32[]{:S(2)}, u32[]{:S(2)}) collective-permute-start(bf16[768,512]{1,0:T(8,128)(2,1)} %slice.51), channel_id=1, source_target_pairs={{0,1},{3,2},{1,3},{2,0},{4,5},{7,6},{5,7},{6,4},{8,9},{11,10},{9,1... | collective-permute-start | bytes 2359304 | tf_op jit(solution)/shard_map/ppermute | solution.py:138
  115.3 4.6 %all-to-all-start.2 = ((bf16[4,2,16,512]{3,2,1,0:T(8,128)(2,1)}), bf16[4,2,16,512]{3,2,1,0:T(8,128)(2,1)S(1)}, u32[]{:S(2)}, u32[]{:S(2)}) async-start(bf16[4,2,16,512]{3,2,1,0:T(8,128)(2,1)} %bitcast.10), calls=%async_computation.2 | async-start | bytes 262144 | tf_op jit(solution)/shard_map/all_to_all | solution.py:207
  120.9 9.3 %collective-permute-done.8 = bf16[1024,512]{1,0:T(8,128)(2,1)} collective-permute-done((bf16[1024,512]{1,0:T(8,128)(2,1)}, bf16[1024,512]{1,0:T(8,128)(2,1)}, u32[]{:S(2)}, u32[]{:S(2)}) %collective-permute-start.8) | collective-permute-done | bytes 1048608 | tf_op jit(solution)/shard_map/ppermute | solution.py:138
  130.2 3.2 %convert_add_fusion = f32[1024,512]{1,0:T(8,128)S(1)} fusion(bf16[1024,512]{1,0:T(8,128)(2,1)} %collective-permute-done.8, bf16[1024,512]{1,0:T(8,128)(2,1)} %collective-permute-done.7, f32[1024,512]{1,0:T(8,128)S(1)} %fusion.1, f32[1024,512]{1,0:T(8,128)S(1)} %copy-done.8, f32[1024,512]{1,0:T(8,128)} %fusion.32), kind=kLoop, calls=%fused_computation.2 | loop fusion | flops 3145728 | bytes 10485760 | tf_op jit(solution)/shard_map/add | solution.py:231
  133.4 23.8 %all-to-all-done.2 = bf16[4,2,16,512]{3,2,1,0:T(8,128)(2,1)S(1)} async-done(((bf16[4,2,16,512]{3,2,1,0:T(8,128)(2,1)}), bf16[4,2,16,512]{3,2,1,0:T(8,128)(2,1)S(1)}, u32[]{:S(2)}, u32[]{:S(2)}) %all-to-all-start.2) | async-done | bytes 131104 | tf_op jit(solution)/shard_map/all_to_all | solution.py:207
  158.1 3.7 %all-to-all-start.3 = ((f32[8,2,16,512]{3,2,1,0:T(8,128)}), f32[8,2,16,512]{3,2,1,0:T(8,128)S(1)}, u32[]{:S(2)}, u32[]{:S(2)}) async-start(f32[8,2,16,512]{3,2,1,0:T(8,128)} %broadcast_in_dim.2), calls=%async_computation.3 | async-start | bytes 1048576 | tf_op jit(solution)/shard_map/all_to_all | solution.py:210
  161.9 2.4 %add_convert_fusion = bf16[1024,512]{1,0:T(8,128)(2,1)} fusion(f32[1024,512]{1,0:T(8,128)S(1)} %convert_add_fusion, bf16[768,512]{1,0:T(8,128)(2,1)} %collective-permute-done.10), kind=kLoop, calls=%fused_computation | loop fusion | flops 1572864 | bytes 3932160 | tf_op jit(solution)/shard_map/convert_element_type | solution.py:234
  164.2 1.7 fusion.23
  166.0 5.6 %all-to-all-done.3 = f32[8,2,16,512]{3,2,1,0:T(8,128)S(1)} async-done(((f32[8,2,16,512]{3,2,1,0:T(8,128)}), f32[8,2,16,512]{3,2,1,0:T(8,128)S(1)}, u32[]{:S(2)}, u32[]{:S(2)}) %all-to-all-start.3) | async-done | bytes 524320 | tf_op jit(solution)/shard_map/all_to_all | solution.py:210
  (80 shorter events, 21.9 us)
Async XLA Ops:
  0.6 35.5 %copy-start = (bf16[512,512]{1,0:T(8,128)(2,1)S(1)}, bf16[512,512]{1,0:T(8,128)(2,1)}, u32[]{:S(2)}) copy-start(bf16[512,512]{1,0:T(8,128)(2,1)} %param.13) | copy-start | bytes 1572868
  0.6 12.4 %copy-start.9 = (bf16[1024,512]{1,0:T(8,128)(2,1)S(1)}, bf16[1024,512]{1,0:T(8,128)(2,1)}, u32[]{:S(2)}) copy-start(bf16[1024,512]{1,0:T(8,128)(2,1)} %param.12) | copy-start | bytes 3145732
  0.7 12.1 %copy-start.16 = (s32[1,1,8,64]{3,2,1,0:T(8,128)S(1)}, s32[1,1,8,64]{3,2,1,0:T(8,128)}, u32[]{:S(2)}) copy-start(s32[1,1,8,64]{3,2,1,0:T(8,128)} %param.21) | copy-start | bytes 6148
  0.7 12.2 %copy-start.20 = (s32[1,1,8]{2,1,0:T(1,128)S(1)}, s32[1,1,8]{2,1,0:T(1,128)}, u32[]{:S(2)}) copy-start(s32[1,1,8]{2,1,0:T(1,128)} %param.22) | copy-start | bytes 100
  0.7 53.4 %collective-permute-start = (bf16[1024,512]{1,0:T(8,128)(2,1)}, bf16[1024,512]{1,0:T(8,128)(2,1)}, u32[]{:S(2)}, u32[]{:S(2)}) collective-permute-start(bf16[1024,512]{1,0:T(8,128)(2,1)} %param.12), channel_id=1, source_target_pairs={{2,0},{1,3},{0,1},{3,2},{6,4},{5,7},{4,5},{7,6},{10,8},{9,11},{8,9... | collective-permute-start | bytes 3145736 | tf_op jit(solution)/shard_map/ppermute | solution.py:138
  6.0 33.6 %collective-permute-start.1 = (bf16[512,512]{1,0:T(8,128)(2,1)}, bf16[512,512]{1,0:T(8,128)(2,1)}, u32[]{:S(2)}, u32[]{:S(2)}) collective-permute-start(bf16[512,512]{1,0:T(8,128)(2,1)} %get-tuple-element.25), channel_id=1, source_target_pairs={{1,0},{2,3},{3,1},{0,2},{5,4},{6,7},{7,5},{4,6},{9,8},{10,11},{11,... | collective-permute-start | bytes 1572872 | tf_op jit(solution)/shard_map/ppermute | solution.py:138
  7.2 51.7 %collective-permute-start.4 = (bf16[512,512]{1,0:T(8,128)(2,1)}, bf16[512,512]{1,0:T(8,128)(2,1)}, u32[]{:S(2)}, u32[]{:S(2)}) collective-permute-start(bf16[512,512]{1,0:T(8,128)(2,1)} %get-tuple-element.25), channel_id=1, source_target_pairs={{1,2},{2,1},{5,6},{6,5},{9,10},{10,9},{13,14},{14,13},{17,18},{18,... | collective-permute-start | bytes 1572872 | tf_op jit(solution)/shard_map/ppermute | solution.py:138
  8.7 42.2 %collective-permute-start.2 = (bf16[512,512]{1,0:T(8,128)(2,1)}, bf16[512,512]{1,0:T(8,128)(2,1)}, u32[]{:S(2)}, u32[]{:S(2)}) collective-permute-start(bf16[512,512]{1,0:T(8,128)(2,1)} %get-tuple-element.24), channel_id=1, source_target_pairs={{1,0},{2,3},{3,1},{0,2},{5,4},{6,7},{7,5},{4,6},{9,8},{10,11},{11,... | collective-permute-start | bytes 1572872 | tf_op jit(solution)/shard_map/ppermute | solution.py:138
  12.1 51.8 %collective-permute-start.6 = (bf16[512,512]{1,0:T(8,128)(2,1)}, bf16[512,512]{1,0:T(8,128)(2,1)S(1)}, u32[]{:S(2)}, u32[]{:S(2)}) collective-permute-start(bf16[512,512]{1,0:T(8,128)(2,1)} %get-tuple-element.24), channel_id=1, source_target_pairs={{1,2},{2,1},{5,6},{6,5},{9,10},{10,9},{13,14},{14,13},{17,18},{18,... | collective-permute-start | bytes 1572872 | tf_op jit(solution)/shard_map/ppermute | solution.py:138
  13.0 5.7 %copy-start.17 = (s32[128]{0:T(128)S(1)}, s32[128]{0:T(128)}, u32[]{:S(2)}) copy-start(s32[128]{0:T(128)} %param.17) | copy-start | bytes 1540
  14.6 22.3 %all-to-all-start = ((bf16[8,64,512]{2,1,0:T(8,128)(2,1)}), bf16[8,64,512]{2,1,0:T(8,128)(2,1)}, u32[]{:S(2)}, u32[]{:S(2)}) async-start(bf16[8,64,512]{2,1,0:T(8,128)(2,1)} %bitcast.1), calls=%async_computation | async-start | bytes 1048576 | tf_op jit(solution)/shard_map/all_to_all | solution.py:175
  31.8 4.3 %copy-start.10 = (bf16[1024,512]{1,0:T(8,128)(2,1)S(1)}, bf16[1024,512]{1,0:T(8,128)(2,1)}, u32[]{:S(2)}) copy-start(bf16[1024,512]{1,0:T(8,128)(2,1)} %param.12) | copy-start | bytes 3145732
  36.8 15.5 %copy-start.12 = (bf16[1024,1024]{1,0:T(8,128)(2,1)S(1)}, bf16[1024,1024]{1,0:T(8,128)(2,1)}, u32[]{:S(2)}) copy-start(bf16[1024,1024]{1,0:T(8,128)(2,1)} %get-tuple-element.17) | copy-start | bytes 6291460
  39.1 15.0 %copy-start.19 = (bf16[1024,1024]{1,0:T(8,128)(2,1)S(1)}, bf16[1024,1024]{1,0:T(8,128)(2,1)}, u32[]{:S(2)}) copy-start(bf16[1024,1024]{1,0:T(8,128)(2,1)} %get-tuple-element.16) | copy-start | bytes 6291460
  39.6 22.4 %collective-permute-start.3 = (bf16[512,512]{1,0:T(8,128)(2,1)}, bf16[512,512]{1,0:T(8,128)(2,1)S(1)}, u32[]{:S(2)}, u32[]{:S(2)}) collective-permute-start(bf16[512,512]{1,0:T(8,128)(2,1)} %collective-permute-done.1), channel_id=1, source_target_pairs={{1,0},{2,3},{5,4},{6,7},{9,8},{10,11},{13,12},{14,15},{17,16},{18,... | collective-permute-start | bytes 1572872 | tf_op jit(solution)/shard_map/ppermute | solution.py:138
  50.8 22.3 %collective-permute-start.5 = (bf16[512,512]{1,0:T(8,128)(2,1)}, bf16[512,512]{1,0:T(8,128)(2,1)S(1)}, u32[]{:S(2)}, u32[]{:S(2)}) collective-permute-start(bf16[512,512]{1,0:T(8,128)(2,1)} %collective-permute-done.2), channel_id=1, source_target_pairs={{1,0},{2,3},{5,4},{6,7},{9,8},{10,11},{13,12},{14,15},{17,16},{18,... | collective-permute-start | bytes 1572872 | tf_op jit(solution)/shard_map/ppermute | solution.py:138
  56.7 5.3 %copy-start.3 = (bf16[1024,1024]{1,0:T(8,128)(2,1)S(1)}, bf16[1024,1024]{1,0:T(8,128)(2,1)}, u32[]{:S(2)}) copy-start(bf16[1024,1024]{1,0:T(8,128)(2,1)} %get-tuple-element.18.dense_ref) | copy-start | bytes 6291460
  62.0 11.1 %copy-start.4 = (bf16[1024,512]{1,0:T(8,128)(2,1)S(1)}, bf16[1024,512]{1,0:T(8,128)(2,1)}, u32[]{:S(2)}) copy-start(bf16[1024,512]{1,0:T(8,128)(2,1)} %cot_ref.1) | copy-start | bytes 3145732
  62.0 11.1 %copy-start.5 = (bf16[512,512]{1,0:T(8,128)(2,1)S(1)}, bf16[512,512]{1,0:T(8,128)(2,1)}, u32[]{:S(2)}) copy-start(bf16[512,512]{1,0:T(8,128)(2,1)} %w_ref.1) | copy-start | bytes 1572868
  77.5 9.7 %copy-start.1 = (bf16[1024,512]{1,0:T(8,128)(2,1)}, bf16[1024,512]{1,0:T(8,128)(2,1)S(1)}, u32[]{:S(2)}) copy-start(bf16[1024,512]{1,0:T(8,128)(2,1)S(1)} %get-tuple-element.20) | copy-start | bytes 3145732
  80.2 6.3 %copy-start.11 = (bf16[1024,512]{1,0:T(8,128)(2,1)S(1)}, bf16[1024,512]{1,0:T(8,128)(2,1)}, u32[]{:S(2)}) copy-start(bf16[1024,512]{1,0:T(8,128)(2,1)} %param.12) | copy-start | bytes 3145732
  80.9 26.8 %collective-permute-start.9 = (bf16[1024,512]{1,0:T(8,128)(2,1)}, bf16[1024,512]{1,0:T(8,128)(2,1)}, u32[]{:S(2)}, u32[]{:S(2)}) collective-permute-start(bf16[1024,512]{1,0:T(8,128)(2,1)} %get-tuple-element.23), channel_id=1, source_target_pairs={{0,1},{3,2},{4,5},{7,6},{8,9},{11,10},{12,13},{15,14},{16,17},{19,... | collective-permute-start | bytes 3145736 | tf_op jit(solution)/shard_map/ppermute | solution.py:138
  84.8 45.4 %collective-permute-start.7 = (bf16[1024,512]{1,0:T(8,128)(2,1)}, bf16[1024,512]{1,0:T(8,128)(2,1)}, u32[]{:S(2)}, u32[]{:S(2)}) collective-permute-start(bf16[1024,512]{1,0:T(8,128)(2,1)} %get-tuple-element.23), channel_id=1, source_target_pairs={{1,2},{2,1},{5,6},{6,5},{9,10},{10,9},{13,14},{14,13},{17,18},{18,... | collective-permute-start | bytes 3145736 | tf_op jit(solution)/shard_map/ppermute | solution.py:138
  89.7 24.8 %all-to-all-start.1 = ((bf16[8,192,512]{2,1,0:T(8,128)(2,1)}), bf16[8,192,512]{2,1,0:T(8,128)(2,1)S(1)}, u32[]{:S(2)}, u32[]{:S(2)}) async-start(bf16[8,192,512]{2,1,0:T(8,128)(2,1)} %pad_maximum_fusion), calls=%async_computation.1 | async-start | bytes 3145728 | tf_op jit(solution)/shard_map/all_to_all | solution.py:202
  93.6 4.5 %copy-start.18 = (bf16[1024,1024]{1,0:T(8,128)(2,1)S(1)}, bf16[1024,1024]{1,0:T(8,128)(2,1)}, u32[]{:S(2)}) copy-start(bf16[1024,1024]{1,0:T(8,128)(2,1)} %get-tuple-element.14) | copy-start | bytes 6291460
  97.6 32.6 %collective-permute-start.8 = (bf16[1024,512]{1,0:T(8,128)(2,1)}, bf16[1024,512]{1,0:T(8,128)(2,1)}, u32[]{:S(2)}, u32[]{:S(2)}) collective-permute-start(bf16[1024,512]{1,0:T(8,128)(2,1)} %convolution_convert_fusion), channel_id=1, source_target_pairs={{0,2},{3,1},{1,0},{2,3},{4,6},{7,5},{5,4},{6,7},{8,10},{11,9},{9,8... | collective-permute-start | bytes 3145736 | tf_op jit(solution)/shard_map/ppermute | solution.py:138
  100.8 6.9 %copy-start.13 = (f32[1024,512]{1,0:T(8,128)S(1)}, f32[1024,512]{1,0:T(8,128)}, u32[]{:S(2)}) copy-start(f32[1024,512]{1,0:T(8,128)} %fusion.33) | copy-start | bytes 6291460
  110.2 51.6 %collective-permute-start.10 = (bf16[768,512]{1,0:T(8,128)(2,1)}, bf16[768,512]{1,0:T(8,128)(2,1)}, u32[]{:S(2)}, u32[]{:S(2)}) collective-permute-start(bf16[768,512]{1,0:T(8,128)(2,1)} %slice.51), channel_id=1, source_target_pairs={{0,1},{3,2},{1,3},{2,0},{4,5},{7,6},{5,7},{6,4},{8,9},{11,10},{9,1... | collective-permute-start | bytes 2359304 | tf_op jit(solution)/shard_map/ppermute | solution.py:138
  113.0 51.3 %collective-permute-start.11 = (bf16[256,512]{1,0:T(8,128)(2,1)S(1)}, bf16[256,512]{1,0:T(8,128)(2,1)}, u32[]{:S(2)}, u32[]{:S(2)}) collective-permute-start(bf16[256,512]{1,0:T(8,128)(2,1)S(1)} %slice.53), channel_id=1, source_target_pairs={{0,1},{3,2},{1,3},{2,0},{4,5},{7,6},{5,7},{6,4},{8,9},{11,10},{9,1... | collective-permute-start | bytes 786440 | tf_op jit(solution)/shard_map/ppermute | solution.py:138
  115.3 41.9 %all-to-all-start.2 = ((bf16[4,2,16,512]{3,2,1,0:T(8,128)(2,1)}), bf16[4,2,16,512]{3,2,1,0:T(8,128)(2,1)S(1)}, u32[]{:S(2)}, u32[]{:S(2)}) async-start(bf16[4,2,16,512]{3,2,1,0:T(8,128)(2,1)} %bitcast.10), calls=%async_computation.2 | async-start | bytes 262144 | tf_op jit(solution)/shard_map/all_to_all | solution.py:207
  119.9 10.3 %copy-start.8 = (f32[1024,512]{1,0:T(8,128)S(1)}, f32[1024,512]{1,0:T(8,128)}, u32[]{:S(2)}) copy-start(f32[1024,512]{1,0:T(8,128)} %fusion.31) | copy-start | bytes 6291460
  158.1 13.4 %all-to-all-start.3 = ((f32[8,2,16,512]{3,2,1,0:T(8,128)}), f32[8,2,16,512]{3,2,1,0:T(8,128)S(1)}, u32[]{:S(2)}, u32[]{:S(2)}) async-start(f32[8,2,16,512]{3,2,1,0:T(8,128)} %broadcast_in_dim.2), calls=%async_computation.3 | async-start | bytes 1048576 | tf_op jit(solution)/shard_map/all_to_all | solution.py:210
  (5 other events, 15.0 us)

commit v3 on v2

--- a/solution.py
+++ b/solution.py
@@ -85,9 +85,7 @@
         agg_ref[at, :] = lax.dot_general(
             grad, w, (((1,), (1,)), ((), ())), preferred_element_type=jnp.float32
         ).astype(jnp.bfloat16)
-    for start in range(0, rows, step):
-        at = slice(start, start + step)
-        term_ref[at, :] = dot_t(dense_ref[:, at], agg_ref[...]).astype(term_ref.dtype)
+    term_ref[...] = dot_t(dense_ref[:, : term_ref.shape[0]], agg_ref[...]).astype(term_ref.dtype)
 
 
 def middle(acc, dense, outer, inner, pre_self, cotangent, w_neigh):
@@ -95,12 +93,13 @@
     vmem = pl.BlockSpec(memory_space=pltpu.VMEM)
     return pl.pallas_call(
         middle_kernel,
-        out_shape=(jax.ShapeDtypeStruct((rows, width), jnp.bfloat16),) * 5,
+        out_shape=(jax.ShapeDtypeStruct((rows, width), jnp.bfloat16),) * 4
+        + (jax.ShapeDtypeStruct((rows // 2, width), jnp.bfloat16),),
         in_specs=[vmem] * 7,
         out_specs=(vmem,) * 5,
         compiler_params=pltpu.CompilerParams(vmem_limit_bytes=40 << 20),
         cost_estimate=pl.CostEstimate(
-            flops=4 * rows * width * (rows + width), bytes_accessed=18 << 20, transcendentals=rows * width
+            flops=2 * rows * width * (rows + width), bytes_accessed=18 << 20, transcendentals=rows * width
         ),
         name="middle",
     )(acc, dense, outer, inner, pre_self, cotangent, w_neigh)
@@ -184,12 +183,16 @@
     summed = summed + dot(part(1)[:, :half], first_a) + dot(part(1)[:, half:], first_b)
     summed = lax.optimization_barrier(summed)
     summed = summed + dot(part(3)[:, :half], third_a + inner_a)
-    out, neighbour, grad_pre, grad_agg, term = middle(
+    out, neighbour, grad_pre, grad_agg, term_a = middle(
         summed, part(3), third_b, inner_b, pre_self, cotangent, w_neigh
     )
 
-    passed = move(term, inward)
-    near = move(term, swap_inner)
+    few = row_count // 2
+    passed_a = move(term_a, inward)
+    near_a = move(term_a, swap_inner)
+    term_b = dot_t(part(3)[:, few:], grad_agg).astype(jnp.bfloat16)
+    passed_b = move(term_b, inward)
+    near_b = move(term_b, swap_inner)
 
     grad_scale = float(row_count * n * dom) ** (-0.5)
     share = width // (n * dom)
@@ -220,14 +223,14 @@
     second_term = dot_t(part(2), grad_agg).astype(jnp.bfloat16)
     second_back = move(second_term, second_out)
     first_term = lax.optimization_barrier(dot_t(part(1), grad_agg))
-    first_term = first_term + passed.astype(jnp.float32)
+    first_term = first_term + jnp.concatenate([passed_a, passed_b]).astype(jnp.float32)
     most = row_count - row_count // 4
     last_a = move(first_term[:most].astype(jnp.bfloat16), first_out)
     last_b = move(first_term[most:].astype(jnp.bfloat16), first_out)
 
     d_x = dot(grad_pre, w_self.T) + dot_t(part(0), grad_agg)
+    d_x = d_x + jnp.concatenate([near_a, near_b]).astype(jnp.float32)
     d_x = d_x + dot_t(selector, returned)
-    d_x = d_x + near.astype(jnp.float32)
     d_x = d_x + second_back.astype(jnp.float32)
     d_x = lax.optimization_barrier(d_x)
     base = jnp.concatenate([last_a.astype(jnp.float32), jnp.zeros((row_count - most, width))])

time: 173 us -> 185 us (1.069)
  starting transfers between devices: 39.1 us -> 44.1 us
  waiting for transfers between devices: 66.5 us -> 70.7 us
  local copies, waits for them, and re-layouts: 5.51 us -> 7.97 us
    ppermute x12 -> x14, starting transfers between devices: 22.8 us -> 27.9 us  [move(): return lax.ppermute(value, 'rep', pairs)]
    ppermute x12 -> x14, waiting for transfers between devices: 36.8 us -> 39.7 us  [move(): return lax.ppermute(value, 'rep', pairs)]
    dot_general x7 -> x8, matrix products: 12.5 us -> 13.6 us  [dot_t(): lax.dot_general(a, b, (((0,), (0,)), ((), ())), preferred_element_type=jn...]
  transfers between devices with their start and end apart: 16 -> 18, of which waited for: 9 -> 8; matrix products, arithmetic and copies ran while one was open for 26% -> 24% of each run, Pallas kernels for 7% -> 7%
where the time goes in v3:
time: 185 us; the launch traced here: 184 us
  waiting for transfers between devices  70.7 us (38%)
  starting transfers between devices  44.1 us (24%)
  matrix products  32.7 us (18%)
  Pallas kernels  15.9 us (9%)
  other arithmetic  11.5 us (6%)
  local copies, waits for them, and re-layouts  7.97 us (4%)
    ppermute x14, waiting for transfers between devices, move(): return lax.ppermute(value, 'rep', pairs)  39.7 us
    ppermute x14, starting transfers between devices, move(): return lax.ppermute(value, 'rep', pairs)  27.9 us
    all_to_all x1, waiting for transfers between devices, per_device(): both = lax.all_to_all(both, 'rep', split_axis=0, concat_axis=0, tiled=True)  25.4 us
    dot_general x9, matrix products, dot(): return jnp.dot(a, b, preferred_element_type=jnp.float32)  19.1 us
    dot_general x8, matrix products, dot_t(): lax.dot_general(a, b, (((0,), (0,)), ((), ())), preferred_element_type=jn...  13.6 us
    pallas_call x1, Pallas kernels, densify(): pl.pallas_call(densify_kernel, out_shape=(jax.ShapeDtypeStruct((rows, row...  12.6 us
    all_to_all x2, starting transfers between devices, per_device(): both = lax.all_to_all(both, 'dom', split_axis=0, concat_axis=0, tiled=True)  8.28 us
    all_to_all x2, waiting for transfers between devices, per_device(): both = lax.all_to_all(both, 'dom', split_axis=0, concat_axis=0, tiled=True)  5.6 us
  transfers between devices with their start and end apart: 18, of which 8 were waited for; matrix products, arithmetic and copies ran while one was open for 24% of the time, Pallas kernels for 7%

profile of v3, /device:TPU:0, one launch (start us, length us, event | category | flops | bytes accessed | tf_op | source)
XLA Modules:
  0.0 184.0 jit_solution(1138808439795932770)
XLA Ops:
  0.7 3.1 %collective-permute-start = (bf16[1024,512]{1,0:T(8,128)(2,1)}, bf16[1024,512]{1,0:T(8,128)(2,1)}, u32[]{:S(2)}, u32[]{:S(2)}) collective-permute-start(bf16[1024,512]{1,0:T(8,128)(2,1)} %param.12), channel_id=1, source_target_pairs={{2,0},{1,3},{0,1},{3,2},{6,4},{5,7},{4,5},{7,6},{10,8},{9,11},{8,9... | collective-permute-start | bytes 3145736 | tf_op jit(solution)/shard_map/ppermute | solution.py:137
  3.8 2.2 %fusion.26 = (bf16[512,512]{1,0:T(8,128)(2,1)}, bf16[512,512]{1,0:T(8,128)(2,1)}) fusion(bf16[1024,512]{1,0:T(8,128)(2,1)} %param.12), kind=kLoop, calls=%fused_computation.43 | loop fusion | bytes 2097152 | tf_op jit(solution)/shard_map/slice | solution.py:140
  8.6 3.4 %collective-permute-start.2 = (bf16[512,512]{1,0:T(8,128)(2,1)}, bf16[512,512]{1,0:T(8,128)(2,1)}, u32[]{:S(2)}, u32[]{:S(2)}) collective-permute-start(bf16[512,512]{1,0:T(8,128)(2,1)} %get-tuple-element.24), channel_id=1, source_target_pairs={{1,0},{2,3},{3,1},{0,2},{5,4},{6,7},{7,5},{4,6},{9,8},{10,11},{11,... | collective-permute-start | bytes 1572872 | tf_op jit(solution)/shard_map/ppermute | solution.py:137
  14.5 4.2 %all-to-all-start = ((bf16[8,64,512]{2,1,0:T(8,128)(2,1)}), bf16[8,64,512]{2,1,0:T(8,128)(2,1)}, u32[]{:S(2)}, u32[]{:S(2)}) async-start(bf16[8,64,512]{2,1,0:T(8,128)(2,1)} %bitcast.1), calls=%async_computation | async-start | bytes 1048576 | tf_op jit(solution)/shard_map/all_to_all | solution.py:174
  19.2 12.6 %densify.1 = (bf16[1024,1024]{1,0:T(8,128)(2,1)}, bf16[1024,1024]{1,0:T(8,128)(2,1)}, bf16[1024,1024]{1,0:T(8,128)(2,1)}, bf16[1024,1024]{1,0:T(8,128)(2,1)}, bf16[1024,512]{1,0:T(8,128)(2,1)}) custom-call(s32[128]{0:T(128)} %local_rows.1, s32[128]{0:T(128)} %fusion.25.local_cols, s32[96]{0:T(128)} %halo_rows.1, s32[96]{0:T(128)} %halo_cols.1, ...), custom_call_target="tpu_custom_call" | custom-call | flops 8388608 | bytes 18874368 | tf_op jit(solution)/shard_map/densify/pallas_call | solution.py:42
  31.8 4.2 %fusion.28 = f32[1024,512]{1,0:T(8,128)} fusion(bf16[1024,1024]{1,0:T(8,128)(2,1)} %get-tuple-element.14, bf16[1024,512]{1,0:T(8,128)(2,1)S(1)} %copy-done.12), kind=kOutput, calls=%fused_computation.45 | convolution fusion | flops 1073741824 | bytes 5242880 | tf_op jit(solution)/shard_map/dot_general | solution.py:59
  36.8 2.2 %fusion.29 = f32[1024,512]{1,0:T(8,128)S(1)} fusion(bf16[1024,512]{1,0:T(8,128)(2,1)} %get-tuple-element.15, bf16[512,512]{1,0:T(8,128)(2,1)} %bitcast.2), kind=kOutput, calls=%fused_computation.46 | convolution fusion | flops 536870912 | bytes 3670016 | tf_op jit(solution)/shard_map/dot_general | solution.py:59
  41.0 9.8 %collective-permute-done.2 = bf16[512,512]{1,0:T(8,128)(2,1)} collective-permute-done((bf16[512,512]{1,0:T(8,128)(2,1)}, bf16[512,512]{1,0:T(8,128)(2,1)}, u32[]{:S(2)}, u32[]{:S(2)}) %collective-permute-start.2) | collective-permute-done | bytes 524320 | tf_op jit(solution)/shard_map/ppermute | solution.py:137
  54.1 2.6 %fusion.30 = f32[1024,512]{1,0:T(8,128)S(1)} fusion(bf16[1024,1024]{1,0:T(8,128)(2,1)S(1)} %copy-done.23, bf16[1024,512]{1,0:T(8,128)(2,1)} %collective-permute-done), kind=kOutput, calls=%fused_computation.47 | convolution fusion | flops 1073741824 | bytes 5242880 | tf_op jit(solution)/shard_map/dot_general | solution.py:59
  56.7 2.0 %add_add_fusion = f32[1024,512]{1,0:T(8,128)S(1)} fusion(f32[1024,512]{1,0:T(8,128)S(1)} %fusion.16, f32[1024,512]{1,0:T(8,128)S(1)} %fusion.30, f32[1024,512]{1,0:T(8,128)S(1)} %copy-done.17, f32[1024,512]{1,0:T(8,128)S(1)} %fusion.29, bf16[512,512]{1,0:T(8,128)(2,1)} %collective-permute-done.2, bf16[1024,1024]{1,0:T(8,128)(2,1)S(1)} %copy-done.15), kind=kOutput, calls=%fused_computation.3 | convolution fusion | flops 538968064 | bytes 12058624 | tf_op jit(solution)/shard_map/dot_general | solution.py:59
  58.8 3.2 %collective-permute-done.3 = bf16[512,512]{1,0:T(8,128)(2,1)S(1)} collective-permute-done((bf16[512,512]{1,0:T(8,128)(2,1)}, bf16[512,512]{1,0:T(8,128)(2,1)S(1)}, u32[]{:S(2)}, u32[]{:S(2)}) %collective-permute-start.3) | collective-permute-done | bytes 524320 | tf_op jit(solution)/shard_map/ppermute | solution.py:137
  63.9 9.2 %collective-permute-done.5.outer_ref = bf16[512,512]{1,0:T(8,128)(2,1)S(1)} collective-permute-done((bf16[512,512]{1,0:T(8,128)(2,1)}, bf16[512,512]{1,0:T(8,128)(2,1)S(1)}, u32[]{:S(2)}, u32[]{:S(2)}) %collective-permute-start.5) | collective-permute-done | bytes 524320 | tf_op jit(solution)/shard_map/ppermute | solution.py:137
  73.1 3.4 %middle.1 = (bf16[1024,512]{1,0:T(8,128)(2,1)}, bf16[1024,512]{1,0:T(8,128)(2,1)S(1)}, bf16[1024,512]{1,0:T(8,128)(2,1)S(1)}, bf16[1024,512]{1,0:T(8,128)(2,1)S(1)}, bf16[512,512]{1,0:T(8,128)(2,1)S(1)}) custom-call(f32[1024,512]{1,0:T(8,128)S(1)} %convolution_add_fusion.acc_ref, bf16[1024,1024]{1,0:T(8,128)(2,1)S(1)} %copy-done.1, ...), custom_call_target="tpu_custom_call" | custom-call | flops 1610612736 | bytes 18874368 | tf_op jit(solution)/shard_map/middle/pallas_call | solution.py:94
  76.5 2.7 %fusion.34 = f32[1024,512]{1,0:T(8,128)} fusion(bf16[1024,1024]{1,0:T(8,128)(2,1)S(1)} %copy-done.15, bf16[1024,512]{1,0:T(8,128)(2,1)S(1)} %get-tuple-element.21), kind=kOutput, calls=%fused_computation.51 | convolution fusion | flops 1073741824 | bytes 5242880 | tf_op jit(solution)/shard_map/dot_general | solution.py:63
  83.7 4.4 %all-to-all-start.1 = ((bf16[8,192,512]{2,1,0:T(8,128)(2,1)}), bf16[8,192,512]{2,1,0:T(8,128)(2,1)}, u32[]{:S(2)}, u32[]{:S(2)}) async-start(bf16[8,192,512]{2,1,0:T(8,128)(2,1)} %pad_maximum_fusion), calls=%async_computation.1 | async-start | bytes 3145728 | tf_op jit(solution)/shard_map/all_to_all | solution.py:205
  88.2 2.9 %convolution_convert_fusion.2 = bf16[512,512]{1,0:T(8,128)(2,1)} fusion(bf16[1024,512]{1,0:T(8,128)(2,1)} %copy-done.7, bf16[1024,1024]{1,0:T(8,128)(2,1)S(1)} %copy-done.2), kind=kOutput, calls=%fused_computation.17 | convolution fusion | flops 537133056 | bytes 2621440 | tf_op jit(solution)/shard_map/dot_general | solution.py:63
  91.1 2.9 %collective-permute-start.11 = (bf16[512,512]{1,0:T(8,128)(2,1)}, bf16[512,512]{1,0:T(8,128)(2,1)S(1)}, u32[]{:S(2)}, u32[]{:S(2)}) collective-permute-start(bf16[512,512]{1,0:T(8,128)(2,1)} %convolution_convert_fusion.2), channel_id=1, source_target_pairs={{0,1},{3,2},{4,5},{7,6},{8,9},{11,10},{12,13},{15,14},{16,17},{19,... | collective-permute-start | bytes 1572872 | tf_op jit(solution)/shard_map/ppermute | solution.py:137
  94.7 5.0 %collective-permute-start.10 = (bf16[512,512]{1,0:T(8,128)(2,1)S(1)}, bf16[512,512]{1,0:T(8,128)(2,1)S(1)}, u32[]{:S(2)}, u32[]{:S(2)}) collective-permute-start(bf16[512,512]{1,0:T(8,128)(2,1)S(1)} %copy-done.10), channel_id=1, source_target_pairs={{0,1},{3,2},{4,5},{7,6},{8,9},{11,10},{12,13},{15,14},{16,17},{19,... | collective-permute-start | bytes 1572872 | tf_op jit(solution)/shard_map/ppermute | solution.py:137
  100.4 2.3 %convolution_convert_fusion = bf16[1024,512]{1,0:T(8,128)(2,1)} fusion(bf16[1024,1024]{1,0:T(8,128)(2,1)S(1)} %copy-done.24, bf16[1024,512]{1,0:T(8,128)(2,1)S(1)} %copy-done.8), kind=kOutput, calls=%fused_computation.10 | convolution fusion | flops 1074266112 | bytes 4194304 | tf_op jit(solution)/shard_map/dot_general | solution.py:63
  102.7 2.0 %collective-permute-start.9 = (bf16[1024,512]{1,0:T(8,128)(2,1)}, bf16[1024,512]{1,0:T(8,128)(2,1)}, u32[]{:S(2)}, u32[]{:S(2)}) collective-permute-start(bf16[1024,512]{1,0:T(8,128)(2,1)} %convolution_convert_fusion), channel_id=1, source_target_pairs={{0,2},{3,1},{1,0},{2,3},{4,6},{7,5},{5,4},{6,7},{8,10},{11,9},{9,8... | collective-permute-start | bytes 3145736 | tf_op jit(solution)/shard_map/ppermute | solution.py:137
  104.7 2.6 %fusion.33 = f32[1024,512]{1,0:T(8,128)} fusion(bf16[1024,1024]{1,0:T(8,128)(2,1)S(1)} %copy-done.22, bf16[1024,512]{1,0:T(8,128)(2,1)S(1)} %copy-done.8), kind=kOutput, calls=%fused_computation.50 | convolution fusion | flops 1073741824 | bytes 5242880 | tf_op jit(solution)/shard_map/dot_general | solution.py:63
  107.4 2.1 %fusion.32 = f32[1024,512]{1,0:T(8,128)} fusion(bf16[1024,512]{1,0:T(8,128)(2,1)S(1)} %copy-done.5, bf16[512,512]{1,0:T(8,128)(2,1)S(1)} %copy-done), kind=kOutput, calls=%fused_computation.49 | convolution fusion | flops 536870912 | bytes 3670016 | tf_op jit(solution)/shard_map/dot_general | solution.py:59
  109.4 8.3 %collective-permute-done.10 = bf16[512,512]{1,0:T(8,128)(2,1)S(1)} collective-permute-done((bf16[512,512]{1,0:T(8,128)(2,1)S(1)}, bf16[512,512]{1,0:T(8,128)(2,1)S(1)}, u32[]{:S(2)}, u32[]{:S(2)}) %collective-permute-start.10) | collective-permute-done | bytes 524320 | tf_op jit(solution)/shard_map/ppermute | solution.py:137
  119.0 2.5 %collective-permute-start.12 = (bf16[768,512]{1,0:T(8,128)(2,1)}, bf16[768,512]{1,0:T(8,128)(2,1)}, u32[]{:S(2)}, u32[]{:S(2)}) collective-permute-start(bf16[768,512]{1,0:T(8,128)(2,1)} %slice.55), channel_id=1, source_target_pairs={{0,1},{3,2},{1,3},{2,0},{4,5},{7,6},{5,7},{6,4},{8,9},{11,10},{9,1... | collective-permute-start | bytes 2359304 | tf_op jit(solution)/shard_map/ppermute | solution.py:137
  122.9 2.1 %slice_reduce_fusion = bf16[128,512]{1,0:T(8,128)(2,1)} fusion(bf16[8,192,512]{2,1,0:T(8,128)(2,1)} %all-to-all-done.1), kind=kLoop, calls=%fused_computation.18 | loop fusion | flops 458752 | bytes 1179648 | tf_op jit(solution)/shard_map/reduce_sum | solution.py:208
  125.0 3.8 %all-to-all-start.2 = ((bf16[4,2,16,512]{3,2,1,0:T(8,128)(2,1)}), bf16[4,2,16,512]{3,2,1,0:T(8,128)(2,1)S(1)}, u32[]{:S(2)}, u32[]{:S(2)}) async-start(bf16[4,2,16,512]{3,2,1,0:T(8,128)(2,1)} %bitcast.10), calls=%async_computation.2 | async-start | bytes 262144 | tf_op jit(solution)/shard_map/all_to_all | solution.py:210
  131.7 8.6 %collective-permute-done.9 = bf16[1024,512]{1,0:T(8,128)(2,1)} collective-permute-done((bf16[1024,512]{1,0:T(8,128)(2,1)}, bf16[1024,512]{1,0:T(8,128)(2,1)}, u32[]{:S(2)}, u32[]{:S(2)}) %collective-permute-start.9) | collective-permute-done | bytes 1048608 | tf_op jit(solution)/shard_map/ppermute | solution.py:137
  140.3 3.0 %convert_add_fusion = f32[1024,512]{1,0:T(8,128)S(1)} fusion(bf16[1024,512]{1,0:T(8,128)(2,1)} %collective-permute-done.9, f32[1024,512]{1,0:T(8,128)S(1)} %fusion.1, f32[1024,512]{1,0:T(8,128)S(1)} %copy-done.11, f32[1024,512]{1,0:T(8,128)} %fusion.33, bf16[512,512]{1,0:T(8,128)(2,1)S(1)} %collective-permute-done.8, bf16[512,512]{1,0:T(8,128)(2,1)} %copy-done.19), kind=kLoop, calls=%fused_computation.2 | loop fusion | flops 4718592 | bytes 10485760 | tf_op jit(solution)/shard_map/add | solution.py:234
  143.3 25.4 %all-to-all-done.2 = bf16[4,2,16,512]{3,2,1,0:T(8,128)(2,1)S(1)} async-done(((bf16[4,2,16,512]{3,2,1,0:T(8,128)(2,1)}), bf16[4,2,16,512]{3,2,1,0:T(8,128)(2,1)S(1)}, u32[]{:S(2)}, u32[]{:S(2)}) %all-to-all-start.2) | async-done | bytes 131104 | tf_op jit(solution)/shard_map/all_to_all | solution.py:210
  169.6 3.8 %all-to-all-start.3 = ((f32[8,2,16,512]{3,2,1,0:T(8,128)}), f32[8,2,16,512]{3,2,1,0:T(8,128)S(1)}, u32[]{:S(2)}, u32[]{:S(2)}) async-start(f32[8,2,16,512]{3,2,1,0:T(8,128)} %broadcast_in_dim.2), calls=%async_computation.3 | async-start | bytes 1048576 | tf_op jit(solution)/shard_map/all_to_all | solution.py:213
  173.4 2.4 %add_convert_fusion = bf16[1024,512]{1,0:T(8,128)(2,1)} fusion(f32[1024,512]{1,0:T(8,128)S(1)} %convert_add_fusion, bf16[768,512]{1,0:T(8,128)(2,1)} %collective-permute-done.12), kind=kLoop, calls=%fused_computation | loop fusion | flops 1572864 | bytes 3932160 | tf_op jit(solution)/shard_map/convert_element_type | solution.py:237
  177.5 5.6 %all-to-all-done.3 = f32[8,2,16,512]{3,2,1,0:T(8,128)S(1)} async-done(((f32[8,2,16,512]{3,2,1,0:T(8,128)}), f32[8,2,16,512]{3,2,1,0:T(8,128)S(1)}, u32[]{:S(2)}, u32[]{:S(2)}) %all-to-all-start.3) | async-done | bytes 524320 | tf_op jit(solution)/shard_map/all_to_all | solution.py:213
  (95 shorter events, 28.4 us)
Async XLA Ops:
  0.6 35.4 %copy-start = (bf16[512,512]{1,0:T(8,128)(2,1)S(1)}, bf16[512,512]{1,0:T(8,128)(2,1)}, u32[]{:S(2)}) copy-start(bf16[512,512]{1,0:T(8,128)(2,1)} %param.13) | copy-start | bytes 1572868
  0.6 12.3 %copy-start.12 = (bf16[1024,512]{1,0:T(8,128)(2,1)S(1)}, bf16[1024,512]{1,0:T(8,128)(2,1)}, u32[]{:S(2)}) copy-start(bf16[1024,512]{1,0:T(8,128)(2,1)} %param.12) | copy-start | bytes 3145732
  0.7 12.1 %copy-start.20 = (s32[1,1,8,64]{3,2,1,0:T(8,128)S(1)}, s32[1,1,8,64]{3,2,1,0:T(8,128)}, u32[]{:S(2)}) copy-start(s32[1,1,8,64]{3,2,1,0:T(8,128)} %param.21) | copy-start | bytes 6148
  0.7 12.1 %copy-start.25 = (s32[1,1,8]{2,1,0:T(1,128)S(1)}, s32[1,1,8]{2,1,0:T(1,128)}, u32[]{:S(2)}) copy-start(s32[1,1,8]{2,1,0:T(1,128)} %param.22) | copy-start | bytes 100
  0.7 53.4 %collective-permute-start = (bf16[1024,512]{1,0:T(8,128)(2,1)}, bf16[1024,512]{1,0:T(8,128)(2,1)}, u32[]{:S(2)}, u32[]{:S(2)}) collective-permute-start(bf16[1024,512]{1,0:T(8,128)(2,1)} %param.12), channel_id=1, source_target_pairs={{2,0},{1,3},{0,1},{3,2},{6,4},{5,7},{4,5},{7,6},{10,8},{9,11},{8,9... | collective-permute-start | bytes 3145736 | tf_op jit(solution)/shard_map/ppermute | solution.py:137
  6.0 33.6 %collective-permute-start.1 = (bf16[512,512]{1,0:T(8,128)(2,1)}, bf16[512,512]{1,0:T(8,128)(2,1)}, u32[]{:S(2)}, u32[]{:S(2)}) collective-permute-start(bf16[512,512]{1,0:T(8,128)(2,1)} %get-tuple-element.25), channel_id=1, source_target_pairs={{1,0},{2,3},{3,1},{0,2},{5,4},{6,7},{7,5},{4,6},{9,8},{10,11},{11,... | collective-permute-start | bytes 1572872 | tf_op jit(solution)/shard_map/ppermute | solution.py:137
  7.1 51.7 %collective-permute-start.4 = (bf16[512,512]{1,0:T(8,128)(2,1)}, bf16[512,512]{1,0:T(8,128)(2,1)}, u32[]{:S(2)}, u32[]{:S(2)}) collective-permute-start(bf16[512,512]{1,0:T(8,128)(2,1)} %get-tuple-element.25), channel_id=1, source_target_pairs={{1,2},{2,1},{5,6},{6,5},{9,10},{10,9},{13,14},{14,13},{17,18},{18,... | collective-permute-start | bytes 1572872 | tf_op jit(solution)/shard_map/ppermute | solution.py:137
  8.6 42.2 %collective-permute-start.2 = (bf16[512,512]{1,0:T(8,128)(2,1)}, bf16[512,512]{1,0:T(8,128)(2,1)}, u32[]{:S(2)}, u32[]{:S(2)}) collective-permute-start(bf16[512,512]{1,0:T(8,128)(2,1)} %get-tuple-element.24), channel_id=1, source_target_pairs={{1,0},{2,3},{3,1},{0,2},{5,4},{6,7},{7,5},{4,6},{9,8},{10,11},{11,... | collective-permute-start | bytes 1572872 | tf_op jit(solution)/shard_map/ppermute | solution.py:137
  12.0 51.8 %collective-permute-start.6 = (bf16[512,512]{1,0:T(8,128)(2,1)}, bf16[512,512]{1,0:T(8,128)(2,1)S(1)}, u32[]{:S(2)}, u32[]{:S(2)}) collective-permute-start(bf16[512,512]{1,0:T(8,128)(2,1)} %get-tuple-element.24), channel_id=1, source_target_pairs={{1,2},{2,1},{5,6},{6,5},{9,10},{10,9},{13,14},{14,13},{17,18},{18,... | collective-permute-start | bytes 1572872 | tf_op jit(solution)/shard_map/ppermute | solution.py:137
  14.5 22.2 %all-to-all-start = ((bf16[8,64,512]{2,1,0:T(8,128)(2,1)}), bf16[8,64,512]{2,1,0:T(8,128)(2,1)}, u32[]{:S(2)}, u32[]{:S(2)}) async-start(bf16[8,64,512]{2,1,0:T(8,128)(2,1)} %bitcast.1), calls=%async_computation | async-start | bytes 1048576 | tf_op jit(solution)/shard_map/all_to_all | solution.py:174
  36.8 15.5 %copy-start.15 = (bf16[1024,1024]{1,0:T(8,128)(2,1)S(1)}, bf16[1024,1024]{1,0:T(8,128)(2,1)}, u32[]{:S(2)}) copy-start(bf16[1024,1024]{1,0:T(8,128)(2,1)} %get-tuple-element.17) | copy-start | bytes 6291460
  39.0 15.1 %copy-start.23 = (bf16[1024,1024]{1,0:T(8,128)(2,1)S(1)}, bf16[1024,1024]{1,0:T(8,128)(2,1)}, u32[]{:S(2)}) copy-start(bf16[1024,1024]{1,0:T(8,128)(2,1)} %get-tuple-element.16) | copy-start | bytes 6291460
  39.6 22.4 %collective-permute-start.3 = (bf16[512,512]{1,0:T(8,128)(2,1)}, bf16[512,512]{1,0:T(8,128)(2,1)S(1)}, u32[]{:S(2)}, u32[]{:S(2)}) collective-permute-start(bf16[512,512]{1,0:T(8,128)(2,1)} %collective-permute-done.1), channel_id=1, source_target_pairs={{1,0},{2,3},{5,4},{6,7},{9,8},{10,11},{13,12},{14,15},{17,16},{18,... | collective-permute-start | bytes 1572872 | tf_op jit(solution)/shard_map/ppermute | solution.py:137
  50.8 22.3 %collective-permute-start.5 = (bf16[512,512]{1,0:T(8,128)(2,1)}, bf16[512,512]{1,0:T(8,128)(2,1)S(1)}, u32[]{:S(2)}, u32[]{:S(2)}) collective-permute-start(bf16[512,512]{1,0:T(8,128)(2,1)} %collective-permute-done.2), channel_id=1, source_target_pairs={{1,0},{2,3},{5,4},{6,7},{9,8},{10,11},{13,12},{14,15},{17,16},{18,... | collective-permute-start | bytes 1572872 | tf_op jit(solution)/shard_map/ppermute | solution.py:137
  62.0 11.1 %copy-start.3 = (bf16[1024,512]{1,0:T(8,128)(2,1)S(1)}, bf16[1024,512]{1,0:T(8,128)(2,1)}, u32[]{:S(2)}) copy-start(bf16[1024,512]{1,0:T(8,128)(2,1)} %cot_ref.1) | copy-start | bytes 3145732
  62.0 11.1 %copy-start.6 = (bf16[512,512]{1,0:T(8,128)(2,1)S(1)}, bf16[512,512]{1,0:T(8,128)(2,1)}, u32[]{:S(2)}) copy-start(bf16[512,512]{1,0:T(8,128)(2,1)} %w_ref.1) | copy-start | bytes 1572868
  83.7 39.2 %all-to-all-start.1 = ((bf16[8,192,512]{2,1,0:T(8,128)(2,1)}), bf16[8,192,512]{2,1,0:T(8,128)(2,1)}, u32[]{:S(2)}, u32[]{:S(2)}) async-start(bf16[8,192,512]{2,1,0:T(8,128)(2,1)} %pad_maximum_fusion), calls=%async_computation.1 | async-start | bytes 3145728 | tf_op jit(solution)/shard_map/all_to_all | solution.py:205
  88.1 6.6 %copy-start.10 = (bf16[512,512]{1,0:T(8,128)(2,1)S(1)}, bf16[512,512]{1,0:T(8,128)(2,1)}, u32[]{:S(2)}) copy-start(bf16[512,512]{1,0:T(8,128)(2,1)} %copy-done.9) | copy-start | bytes 1572868
  88.1 12.3 %copy-start.8 = (bf16[1024,512]{1,0:T(8,128)(2,1)S(1)}, bf16[1024,512]{1,0:T(8,128)(2,1)}, u32[]{:S(2)}) copy-start(bf16[1024,512]{1,0:T(8,128)(2,1)} %copy-done.7) | copy-start | bytes 3145732
  88.1 12.3 %copy-start.24 = (bf16[1024,1024]{1,0:T(8,128)(2,1)S(1)}, bf16[1024,1024]{1,0:T(8,128)(2,1)}, u32[]{:S(2)}) copy-start(bf16[1024,1024]{1,0:T(8,128)(2,1)} %get-tuple-element.16) | copy-start | bytes 6291460
  91.1 18.4 %collective-permute-start.11 = (bf16[512,512]{1,0:T(8,128)(2,1)}, bf16[512,512]{1,0:T(8,128)(2,1)S(1)}, u32[]{:S(2)}, u32[]{:S(2)}) collective-permute-start(bf16[512,512]{1,0:T(8,128)(2,1)} %convolution_convert_fusion.2), channel_id=1, source_target_pairs={{0,1},{3,2},{4,5},{7,6},{8,9},{11,10},{12,13},{15,14},{16,17},{19,... | collective-permute-start | bytes 1572872 | tf_op jit(solution)/shard_map/ppermute | solution.py:137
  94.0 36.9 %collective-permute-start.8 = (bf16[512,512]{1,0:T(8,128)(2,1)}, bf16[512,512]{1,0:T(8,128)(2,1)S(1)}, u32[]{:S(2)}, u32[]{:S(2)}) collective-permute-start(bf16[512,512]{1,0:T(8,128)(2,1)} %convolution_convert_fusion.2), channel_id=1, source_target_pairs={{1,2},{2,1},{5,6},{6,5},{9,10},{10,9},{13,14},{14,13},{17,18},{18,... | collective-permute-start | bytes 1572872 | tf_op jit(solution)/shard_map/ppermute | solution.py:137
  94.7 10.0 %copy-start.22 = (bf16[1024,1024]{1,0:T(8,128)(2,1)S(1)}, bf16[1024,1024]{1,0:T(8,128)(2,1)}, u32[]{:S(2)}) copy-start(bf16[1024,1024]{1,0:T(8,128)(2,1)} %get-tuple-element.14) | copy-start | bytes 6291460
  94.7 23.0 %collective-permute-start.10 = (bf16[512,512]{1,0:T(8,128)(2,1)S(1)}, bf16[512,512]{1,0:T(8,128)(2,1)S(1)}, u32[]{:S(2)}, u32[]{:S(2)}) collective-permute-start(bf16[512,512]{1,0:T(8,128)(2,1)S(1)} %copy-done.10), channel_id=1, source_target_pairs={{0,1},{3,2},{4,5},{7,6},{8,9},{11,10},{12,13},{15,14},{16,17},{19,... | collective-permute-start | bytes 1572872 | tf_op jit(solution)/shard_map/ppermute | solution.py:137
  99.7 31.2 %collective-permute-start.7 = (bf16[512,512]{1,0:T(8,128)(2,1)S(1)}, bf16[512,512]{1,0:T(8,128)(2,1)S(1)}, u32[]{:S(2)}, u32[]{:S(2)}) collective-permute-start(bf16[512,512]{1,0:T(8,128)(2,1)S(1)} %copy-done.10), channel_id=1, source_target_pairs={{1,2},{2,1},{5,6},{6,5},{9,10},{10,9},{13,14},{14,13},{17,18},{18,... | collective-permute-start | bytes 1572872 | tf_op jit(solution)/shard_map/ppermute | solution.py:137
  102.7 37.6 %collective-permute-start.9 = (bf16[1024,512]{1,0:T(8,128)(2,1)}, bf16[1024,512]{1,0:T(8,128)(2,1)}, u32[]{:S(2)}, u32[]{:S(2)}) collective-permute-start(bf16[1024,512]{1,0:T(8,128)(2,1)} %convolution_convert_fusion), channel_id=1, source_target_pairs={{0,2},{3,1},{1,0},{2,3},{4,6},{7,5},{5,4},{6,7},{8,10},{11,9},{9,8... | collective-permute-start | bytes 3145736 | tf_op jit(solution)/shard_map/ppermute | solution.py:137
  107.4 10.3 %copy-start.16 = (f32[1024,512]{1,0:T(8,128)S(1)}, f32[1024,512]{1,0:T(8,128)}, u32[]{:S(2)}) copy-start(f32[1024,512]{1,0:T(8,128)} %fusion.34) | copy-start | bytes 6291460
  119.0 54.4 %collective-permute-start.12 = (bf16[768,512]{1,0:T(8,128)(2,1)}, bf16[768,512]{1,0:T(8,128)(2,1)}, u32[]{:S(2)}, u32[]{:S(2)}) collective-permute-start(bf16[768,512]{1,0:T(8,128)(2,1)} %slice.55), channel_id=1, source_target_pairs={{0,1},{3,2},{1,3},{2,0},{4,5},{7,6},{5,7},{6,4},{8,9},{11,10},{9,1... | collective-permute-start | bytes 2359304 | tf_op jit(solution)/shard_map/ppermute | solution.py:137
  121.6 54.3 %collective-permute-start.13 = (bf16[256,512]{1,0:T(8,128)(2,1)S(1)}, bf16[256,512]{1,0:T(8,128)(2,1)}, u32[]{:S(2)}, u32[]{:S(2)}) collective-permute-start(bf16[256,512]{1,0:T(8,128)(2,1)S(1)} %slice.57), channel_id=1, source_target_pairs={{0,1},{3,2},{1,3},{2,0},{4,5},{7,6},{5,7},{6,4},{8,9},{11,10},{9,1... | collective-permute-start | bytes 786440 | tf_op jit(solution)/shard_map/ppermute | solution.py:137
  125.0 43.7 %all-to-all-start.2 = ((bf16[4,2,16,512]{3,2,1,0:T(8,128)(2,1)}), bf16[4,2,16,512]{3,2,1,0:T(8,128)(2,1)S(1)}, u32[]{:S(2)}, u32[]{:S(2)}) async-start(bf16[4,2,16,512]{3,2,1,0:T(8,128)(2,1)} %bitcast.10), calls=%async_computation.2 | async-start | bytes 262144 | tf_op jit(solution)/shard_map/all_to_all | solution.py:210
  128.7 11.6 %copy-start.11 = (f32[1024,512]{1,0:T(8,128)S(1)}, f32[1024,512]{1,0:T(8,128)}, u32[]{:S(2)}) copy-start(f32[1024,512]{1,0:T(8,128)} %fusion.32) | copy-start | bytes 6291460
  169.6 13.6 %all-to-all-start.3 = ((f32[8,2,16,512]{3,2,1,0:T(8,128)}), f32[8,2,16,512]{3,2,1,0:T(8,128)S(1)}, u32[]{:S(2)}, u32[]{:S(2)}) async-start(f32[8,2,16,512]{3,2,1,0:T(8,128)} %broadcast_in_dim.2), calls=%async_computation.3 | async-start | bytes 1048576 | tf_op jit(solution)/shard_map/all_to_all | solution.py:213
  (12 other events, 41.7 us)
